TPU v7x, 128 devices: a whole 4x4x4 slice. The times are simulated.
128 devices in a mesh: ctx: 32 (over x, y, core), head: 4 (over z).
Axes of the slice: x: 4, y: 4, z: 4, core: 2. Of those that a mesh axis runs over, the one named last changes fastest.
Arguments:
- queries: bfloat16 [49152, 1024], P(('ctx', 'head')), may hold values from -30 to 30
- keys: bfloat16 [49152, 1024], P(('ctx', 'head')), may hold values from -30 to 30
- values: bfloat16 [49152, 1024], P(('ctx', 'head')), may hold values from -6 to 6
- directions: bfloat16 [49152, 1024], P(('ctx', 'head')), may hold values from -64 to 64
Outputs:
- attended: bfloat16 [49152, 1024], P(('ctx', 'head'))
All inputs are finite; a program needn't handle non-finite values.
Results may differ from a plain program's by a relative error of at most 0.013.
The roundings to bfloat16 on the way count: a program that leaves them out, or rounds other values in their place, can miss the bound.
Values may be sent and summed in bfloat16 or wider, within the bound.
No kernel may reach another device: no remote copies, remote signals or barrier semaphores. Data moves between devices by JAX's collectives and lax.ppermute only.
A program may use at most 64 MiB of HBM per device.

v0:
```python
import math

import jax
import jax.numpy as jnp
from jax import lax
from jax.sharding import PartitionSpec as P

DH = 128
HOPS = 3
SUB = 128


highest = lax.Precision.HIGHEST
negative = -1e30


def shifted(value, axis, by):
    length = lax.axis_size(axis)
    return lax.ppermute(value, axis, [(i, (i + by) % length) for i in range(length)])


def unit_rows(raw):
    values32 = raw.astype(jnp.float32)
    return values32 / jnp.sqrt(jnp.sum(values32 * values32, axis=-1, keepdims=True) + 1e-06)


def invert_upper(matrix):
    order = matrix.shape[-1]
    if order == 1:
        return 1.0 / matrix
    half = order // 2
    both = invert_upper(jnp.stack([matrix[..., :half, :half], matrix[..., half:, half:]], 0))
    first_inv = both[0]
    second_inv = both[1]
    corner = jnp.matmul(
        jnp.matmul(first_inv, matrix[..., :half, half:], precision=highest),
        second_inv,
        precision=highest,
    )
    upper_rows = jnp.concatenate([first_inv, -corner], axis=-1)
    lower_rows = jnp.concatenate([jnp.zeros_like(corner), second_inv], axis=-1)
    return jnp.concatenate([upper_rows, lower_rows], axis=-2)


def block_product(normals, inputs):
    length = normals.shape[0]
    width = normals.shape[1]
    gram = jnp.dot(normals, normals.T, precision=highest)
    inverse_t = 0.5 * jnp.eye(length, dtype=jnp.float32) + jnp.triu(gram, 1)
    factor = invert_upper(inverse_t)
    upper = jnp.triu(jnp.ones((length, length), jnp.float32))
    results = []
    for vectors in inputs:
        project = jnp.dot(normals, vectors.T, precision=highest) * upper
        weights = jnp.dot(factor, project, precision=highest)
        results.append(vectors - jnp.dot(weights.T, normals, precision=highest))
    solved = jnp.dot(factor, normals, precision=highest)
    whole = jnp.eye(width, dtype=jnp.float32) - jnp.dot(normals.T, solved, precision=highest)
    return (results, whole)


def shard_frames(raw_dirs, queries, keys):
    length, width = queries.shape
    blocks = length // SUB
    normals = unit_rows(raw_dirs).reshape(blocks, SUB, width)
    query_blocks = queries.astype(jnp.float32).reshape(blocks, SUB, width)
    key_blocks = keys.astype(jnp.float32).reshape(blocks, SUB, width)

    def advance(frame, item):
        moved, whole = block_product(item[0], (item[1], item[2]))
        frame_low = frame.astype(jnp.bfloat16)
        outputs = (
            jnp.dot(moved[0].astype(jnp.bfloat16), frame_low.T, preferred_element_type=jnp.float32),
            jnp.dot(moved[1].astype(jnp.bfloat16), frame_low.T, preferred_element_type=jnp.float32),
        )
        return (jnp.dot(frame, whole, precision=highest), outputs)

    final, turned = lax.scan(
        advance, jnp.eye(width, dtype=jnp.float32), (normals, query_blocks, key_blocks)
    )
    return (
        final,
        turned[0].reshape(length, width),
        turned[1].reshape(length, width).astype(jnp.bfloat16),
    )


def attend(query, keys, values, causal):
    heads, length, width = query.shape
    span = min(512, length)
    number = length // span
    scale = 1.0 / math.sqrt(width)
    blocks = query.reshape(heads, number, span, width).transpose(1, 0, 2, 3)
    key_index = jnp.arange(keys.shape[1])

    def one_block(item):
        block, start = item
        scores = jnp.einsum("hqd,hkd->hqk", block, keys, preferred_element_type=jnp.float32) * scale
        if causal:
            query_index = start * span + jnp.arange(span)
            scores = jnp.where(query_index[:, None] >= key_index[None, :], scores, negative)
        best = jnp.max(scores, axis=-1)
        weights = jnp.exp(scores - best[..., None])
        total = jnp.sum(weights, axis=-1)
        output = jnp.einsum(
            "hqk,hkd->hqd", weights.astype(jnp.bfloat16), values, preferred_element_type=jnp.float32
        )
        return (best, output, total)

    best, output, total = lax.map(one_block, (blocks, jnp.arange(number)))
    return (
        best.transpose(1, 0, 2).reshape(heads, length),
        output.transpose(1, 0, 2, 3).reshape(heads, length, width),
        total.transpose(1, 0, 2).reshape(heads, length),
    )


def combine(state, block, valid):
    best, total_o, total_l = state
    block_best, block_o, block_l = block
    top = jnp.maximum(best, block_best)
    old_scale = jnp.exp(best - top)
    new_scale = jnp.exp(block_best - top)
    merged_o = total_o * old_scale[..., None] + block_o * new_scale[..., None]
    merged_l = total_l * old_scale + block_l * new_scale
    return (
        jnp.where(valid, top, best),
        jnp.where(valid, merged_o, total_o),
        jnp.where(valid, merged_l, total_l),
    )


def body(queries, keys, values, directions):
    local_q, local_k, local_v, local_w = (
        lax.all_to_all(queries, "head", split_axis=1, concat_axis=0, tiled=True),
        lax.all_to_all(keys, "head", split_axis=1, concat_axis=0, tiled=True),
        lax.all_to_all(values, "head", split_axis=1, concat_axis=0, tiled=True),
        lax.all_to_all(directions, "head", split_axis=1, concat_axis=0, tiled=True),
    )
    rows = local_q.shape[0]
    heads_here = local_q.shape[1] // DH

    def split_heads(array):
        return array.reshape(rows, heads_here, DH).transpose(1, 0, 2)

    frames, turned, key_turned = jax.vmap(shard_frames)(
        split_heads(local_w), split_heads(local_q), split_heads(local_k)
    )
    frames_low = frames.astype(jnp.bfloat16)
    value_heads = split_heads(local_v)
    state = attend(turned.astype(jnp.bfloat16), key_turned, value_heads, True)
    position = lax.axis_index("ctx")
    number = lax.axis_size("ctx")
    moving = turned
    best, total_o, total_l = state
    for distance in range(1, HOPS + 1):
        moving, total_o, best, total_l = shifted((moving, total_o, best, total_l), "ctx", -1)
        moving = jnp.einsum(
            "htd,hed->hte",
            moving.astype(jnp.bfloat16),
            frames_low,
            preferred_element_type=jnp.float32,
        )
        block = attend(moving.astype(jnp.bfloat16), key_turned, value_heads, False)
        best, total_o, total_l = combine(
            (best, total_o, total_l), block, position + distance < number
        )
    finished = (total_o / total_l[..., None]).astype(jnp.bfloat16)
    finished = shifted(finished, "ctx", HOPS)
    merged = finished.transpose(1, 0, 2).reshape(rows, heads_here * DH)
    return lax.all_to_all(merged, "head", split_axis=0, concat_axis=1, tiled=True)


def solution(mesh):
    return jax.shard_map(
        body,
        mesh=mesh,
        in_specs=(
            P(("ctx", "head"), None),
            P(("ctx", "head"), None),
            P(("ctx", "head"), None),
            P(("ctx", "head"), None),
        ),
        out_specs=P(("ctx", "head"), None),
        check_vma=False,
    )
```

profile of v0, /device:TPU:0, one launch (start us, length us, event | category | flops | bytes accessed | tf_op | source)
XLA Modules:
  0.0 445.8 jit_solution(15689126845406524768)
XLA Ops:
  2.1 5.5 %all-to-all-start = ((bf16[384,4,256]{2,0,1:T(8,128)(2,1)}), bf16[384,4,256]{2,0,1:T(8,128)(2,1)S(1)}, u32[]{:S(2)}, u32[]{:S(2)}) async-start(bf16[384,4,256]{2,0,1:T(8,128)(2,1)} %bitcast.346), calls=%async_computation | async-start | bytes 1572864 | tf_op jit(solution)/shard_map/all_to_all | solution.py:138
  10.6 9.4 %all-to-all-done = bf16[384,4,256]{2,0,1:T(8,128)(2,1)S(1)} async-done(((bf16[384,4,256]{2,0,1:T(8,128)(2,1)}), bf16[384,4,256]{2,0,1:T(8,128)(2,1)S(1)}, u32[]{:S(2)}, u32[]{:S(2)}) %all-to-all-start) | async-done | bytes 786464 | tf_op jit(solution)/shard_map/all_to_all | solution.py:138
  20.0 4.2 all-to-all-start.1
  25.1 2.6 fusion.156
  28.0 7.7 %all-to-all-done.1 = bf16[384,4,256]{2,0,1:T(8,128)(2,1)} async-done(((bf16[384,4,256]{2,0,1:T(8,128)(2,1)}), bf16[384,4,256]{2,0,1:T(8,128)(2,1)}, u32[]{:S(2)}, u32[]{:S(2)}) %all-to-all-start.1) | async-done | bytes 786464 | tf_op jit(solution)/shard_map/all_to_all | solution.py:135
  35.7 4.2 all-to-all-start.2
  45.1 2.7 copy.103
  50.2 4.7 %all-to-all-start.3 = ((bf16[384,4,256]{2,0,1:T(8,128)(2,1)}), bf16[384,4,256]{2,0,1:T(8,128)(2,1)}, u32[]{:S(2)}, u32[]{:S(2)}) async-start(bf16[384,4,256]{2,0,1:T(8,128)(2,1)} %bitcast.343), calls=%async_computation.3 | async-start | bytes 1572864 | tf_op jit(solution)/shard_map/all_to_all | solution.py:137
  59.6 217.0 %while.71 = (s32[]{:T(128)}, f32[2,128,128]{1,2,0:T(8,128)S(1)}, bf16[12,2,128,128]{3,2,0,1:T(8,128)(2,1)}, bf16[12,2,128,128]{3,2,1,0:T(8,128)(2,1)}, f32[12,2,...) while((s32[]{:T(128)}, f32[2,128,128]{1,2,0:T(8,128)S(1)}, ...), condition=%wide.region_2.3_spmd, body=%wide.region_1.2_spmd.sunk | while | flops 537905536 | bytes 20356264 | solution.py:78
  282.7 26.2 %while.75 = (s32[]{:T(128)}, f32[3,2,512]{2,1,0:T(2,128)S(1)}, f32[3,2,512,128]{3,2,0,1:T(8,128)}, f32[3,2,512]{2,1,0:T(2,128)S(1)}, s32[3]{0:T(128)S(1)}, /*ind...) while((s32[]{:T(128)}, f32[3,2,512]{2,1,0:T(2,128)S(1)}, ...), condition=%wide.region_6.7_spmd.clone, body=%wide.region_3.6_spmd.clone.sunk | while | flops 823392768 | bytes 24416404 | solution.py:110
  284.5 2.5 fusion.351
  289.0 2.4 fusion.353
  293.3 2.5 fusion.351
  297.8 2.4 fusion.353
  302.0 2.5 fusion.351
  306.5 2.4 fusion.353
  308.9 4.1 collective-permute-start
  316.5 10.6 %while.72 = (s32[]{:T(128)}, f32[3,2,512]{2,1,0:T(2,128)S(1)}, f32[3,2,512,128]{3,2,0,1:T(8,128)S(1)}, f32[3,2,512]{2,1,0:T(2,128)S(1)}, bf16[3,2,512,128]{3,2,1...) while((s32[]{:T(128)}, f32[3,2,512]{2,1,0:T(2,128)S(1)}, ...), condition=%wide.region_10.11_spmd, body=%wide.region_7.10_spmd.sunk | while | flops 817887232 | bytes 24412292 | solution.py:110
  327.1 4.2 collective-permute-done.9
  331.5 5.3 %collective-permute-start.10 = (f32[2,1536]{1,0:T(2,128)S(1)}, f32[2,1536]{1,0:T(2,128)S(1)}, u32[]{:S(2)}, u32[]{:S(2)}) collective-permute-start(f32[2,1536]{1,0:T(2,128)S(1)} %get-tuple-element.395), channel_id=1, source_target_pairs={{0,124},{4,0},{8,4},{12,8},{16,12},{20,16},{24,20},{28,24},{32,28}... | collective-permute-start | bytes 36872 | tf_op jit(solution)/shard_map/ppermute | solution.py:19
  336.8 3.0 fusion.155
  342.3 5.4 %collective-permute-start.8 = (bf16[2,1536,128]{2,1,0:T(8,128)(2,1)}, bf16[2,1536,128]{2,1,0:T(8,128)(2,1)}, u32[]{:S(2)}, u32[]{:S(2)}) collective-permute-start(bf16[2,1536,128]{2,1,0:T(8,128)(2,1)} %fusion.159), channel_id=1, source_target_pairs={{0,124},{4,0},{8,4},{12,8},{16,12},{20,16},{24,20},{28,24},{32,28}... | collective-permute-start | bytes 2359304 | tf_op jit(solution)/shard_map/ppermute | solution.py:19
  349.1 10.6 %while.73 = (s32[]{:T(128)}, f32[3,2,512]{2,1,0:T(2,128)S(1)}, f32[3,2,512,128]{3,2,0,1:T(8,128)S(1)}, f32[3,2,512]{2,1,0:T(2,128)S(1)}, bf16[3,2,512,128]{3,2,1...) while((s32[]{:T(128)}, f32[3,2,512]{2,1,0:T(2,128)S(1)}, ...), condition=%wide.region_14.15_spmd, body=%wide.region_11.14_spmd.sunk | while | flops 817887232 | bytes 24412292 | solution.py:110
  359.9 6.6 %collective-permute-done.8 = bf16[2,1536,128]{2,1,0:T(8,128)(2,1)} collective-permute-done((bf16[2,1536,128]{2,1,0:T(8,128)(2,1)}, bf16[2,1536,128]{2,1,0:T(8,128)(2,1)}, u32[]{:S(2)}, u32[]{:S(2)}) %collective-permute-start.8) | collective-permute-done | bytes 786464 | tf_op jit(solution)/shard_map/ppermute | solution.py:19
  368.1 3.0 fusion.153
  371.1 5.2 %collective-permute-start.6 = (f32[2,1536,128]{2,1,0:T(8,128)}, f32[2,1536,128]{2,1,0:T(8,128)}, u32[]{:S(2)}, u32[]{:S(2)}) collective-permute-start(f32[2,1536,128]{2,1,0:T(8,128)} %fusion.153), channel_id=1, source_target_pairs={{0,124},{4,0},{8,4},{12,8},{16,12},{20,16},{24,20},{28,24},{32,28}... | collective-permute-start | bytes 4718600 | tf_op jit(solution)/shard_map/ppermute | solution.py:19
  376.5 10.5 %while.74 = (s32[]{:T(128)}, f32[3,2,512]{2,1,0:T(2,128)S(1)}, f32[3,2,512,128]{3,2,0,1:T(8,128)S(1)}, f32[3,2,512]{2,1,0:T(2,128)S(1)}, bf16[3,2,512,128]{3,2,1...) while((s32[]{:T(128)}, f32[3,2,512]{2,1,0:T(2,128)S(1)}, ...), condition=%wide.region_18.19_spmd, body=%wide.region_15.18_spmd.sunk | while | flops 817887232 | bytes 24412292 | solution.py:110
  387.1 7.5 %collective-permute-done.6 = f32[2,1536,128]{2,1,0:T(8,128)} collective-permute-done((f32[2,1536,128]{2,1,0:T(8,128)}, f32[2,1536,128]{2,1,0:T(8,128)}, u32[]{:S(2)}, u32[]{:S(2)}) %collective-permute-start.6) | collective-permute-done | bytes 1572896 | tf_op jit(solution)/shard_map/ppermute | solution.py:19
  394.6 3.1 fusion.157
  398.0 22.3 %collective-permute-done.12 = bf16[2,1536,128]{2,1,0:T(8,128)(2,1)S(1)} collective-permute-done((bf16[2,1536,128]{2,1,0:T(8,128)(2,1)S(1)}, bf16[2,1536,128]{2,1,0:T(8,128)(2,1)S(1)}, u32[]{:S(2)}, u32[]{:S(2)}) %collective-permute-start.12) | collective-permute-done | bytes 786464 | tf_op jit(solution)/shard_map/ppermute | solution.py:19
  420.3 6.5 %copy.127 = bf16[1536,2,128]{2,1,0:T(2,128)(2,1)S(1)} copy(bf16[1536,2,128]{2,0,1:T(8,128)(2,1)S(1)} %bitcast.522) | data formatting | bytes 1572864 | tf_op jit(solution)/shard_map/transpose | solution.py:170
  427.3 16.6 %all_to_all.74 = bf16[4,384,256]{2,1,0:T(8,128)(2,1)S(1)} all-to-all(bf16[4,384,256]{2,1,0:T(8,128)(2,1)S(1)} %all_to_all.65), channel_id=1, replica_groups=mesh['ctx'=32,'head'=4] {'head'}, dimensions={0} | all-to-all | bytes 1572864 | tf_op jit(solution)/shard_map/all_to_all | solution.py:171
  (887 shorter events, 289.7 us)
Async XLA Ops:
  0.0 7.7 %copy-start.2 = (bf16[384,1024]{1,0:T(8,128)(2,1)S(1)}, bf16[384,1024]{1,0:T(8,128)(2,1)}, u32[]{:S(2)}) copy-start(bf16[384,1024]{1,0:T(8,128)(2,1)} %param.14) | copy-start | bytes 2359300
  2.1 6.5 %copy-start.3 = (bf16[384,1024]{1,0:T(8,128)(2,1)S(1)}, bf16[384,1024]{1,0:T(8,128)(2,1)}, u32[]{:S(2)}) copy-start(bf16[384,1024]{1,0:T(8,128)(2,1)} %param.15) | copy-start | bytes 2359300
  2.1 17.8 %all-to-all-start = ((bf16[384,4,256]{2,0,1:T(8,128)(2,1)}), bf16[384,4,256]{2,0,1:T(8,128)(2,1)S(1)}, u32[]{:S(2)}, u32[]{:S(2)}) async-start(bf16[384,4,256]{2,0,1:T(8,128)(2,1)} %bitcast.346), calls=%async_computation | async-start | bytes 1572864 | tf_op jit(solution)/shard_map/all_to_all | solution.py:138
  20.0 15.7 %all-to-all-start.1 = ((bf16[384,4,256]{2,0,1:T(8,128)(2,1)}), bf16[384,4,256]{2,0,1:T(8,128)(2,1)}, u32[]{:S(2)}, u32[]{:S(2)}) async-start(bf16[384,4,256]{2,0,1:T(8,128)(2,1)} %bitcast.345), calls=%async_computation.1 | async-start | bytes 1572864 | tf_op jit(solution)/shard_map/all_to_all | solution.py:135
  35.7 14.5 %all-to-all-start.2 = ((bf16[384,4,256]{2,0,1:T(8,128)(2,1)}), bf16[384,4,256]{2,0,1:T(8,128)(2,1)}, u32[]{:S(2)}, u32[]{:S(2)}) async-start(bf16[384,4,256]{2,0,1:T(8,128)(2,1)} %bitcast.344), calls=%async_computation.2 | async-start | bytes 1572864 | tf_op jit(solution)/shard_map/all_to_all | solution.py:136
  50.2 227.6 %all-to-all-start.3 = ((bf16[384,4,256]{2,0,1:T(8,128)(2,1)}), bf16[384,4,256]{2,0,1:T(8,128)(2,1)}, u32[]{:S(2)}, u32[]{:S(2)}) async-start(bf16[384,4,256]{2,0,1:T(8,128)(2,1)} %bitcast.343), calls=%async_computation.3 | async-start | bytes 1572864 | tf_op jit(solution)/shard_map/all_to_all | solution.py:137
  72.7 5.0 %copy-start.1 = (f32[12,2,128,128]{3,2,0,1:T(8,128)S(1)}, f32[12,2,128,128]{3,2,0,1:T(8,128)}, u32[]{:S(2)}) copy-start(f32[12,2,128,128]{3,2,0,1:T(8,128)} %copy-done) | copy-start | bytes 4718596 | tf_op jit(solution)/shard_map/vmap()/while
  90.8 5.0 %copy-start.1 = (f32[12,2,128,128]{3,2,0,1:T(8,128)S(1)}, f32[12,2,128,128]{3,2,0,1:T(8,128)}, u32[]{:S(2)}) copy-start(f32[12,2,128,128]{3,2,0,1:T(8,128)} %copy-done) | copy-start | bytes 4718596 | tf_op jit(solution)/shard_map/vmap()/while
  108.9 5.0 %copy-start.1 = (f32[12,2,128,128]{3,2,0,1:T(8,128)S(1)}, f32[12,2,128,128]{3,2,0,1:T(8,128)}, u32[]{:S(2)}) copy-start(f32[12,2,128,128]{3,2,0,1:T(8,128)} %copy-done) | copy-start | bytes 4718596 | tf_op jit(solution)/shard_map/vmap()/while
  127.0 5.0 %copy-start.1 = (f32[12,2,128,128]{3,2,0,1:T(8,128)S(1)}, f32[12,2,128,128]{3,2,0,1:T(8,128)}, u32[]{:S(2)}) copy-start(f32[12,2,128,128]{3,2,0,1:T(8,128)} %copy-done) | copy-start | bytes 4718596 | tf_op jit(solution)/shard_map/vmap()/while
  145.1 5.0 %copy-start.1 = (f32[12,2,128,128]{3,2,0,1:T(8,128)S(1)}, f32[12,2,128,128]{3,2,0,1:T(8,128)}, u32[]{:S(2)}) copy-start(f32[12,2,128,128]{3,2,0,1:T(8,128)} %copy-done) | copy-start | bytes 4718596 | tf_op jit(solution)/shard_map/vmap()/while
  163.1 5.0 %copy-start.1 = (f32[12,2,128,128]{3,2,0,1:T(8,128)S(1)}, f32[12,2,128,128]{3,2,0,1:T(8,128)}, u32[]{:S(2)}) copy-start(f32[12,2,128,128]{3,2,0,1:T(8,128)} %copy-done) | copy-start | bytes 4718596 | tf_op jit(solution)/shard_map/vmap()/while
  181.2 5.0 %copy-start.1 = (f32[12,2,128,128]{3,2,0,1:T(8,128)S(1)}, f32[12,2,128,128]{3,2,0,1:T(8,128)}, u32[]{:S(2)}) copy-start(f32[12,2,128,128]{3,2,0,1:T(8,128)} %copy-done) | copy-start | bytes 4718596 | tf_op jit(solution)/shard_map/vmap()/while
  199.3 5.0 %copy-start.1 = (f32[12,2,128,128]{3,2,0,1:T(8,128)S(1)}, f32[12,2,128,128]{3,2,0,1:T(8,128)}, u32[]{:S(2)}) copy-start(f32[12,2,128,128]{3,2,0,1:T(8,128)} %copy-done) | copy-start | bytes 4718596 | tf_op jit(solution)/shard_map/vmap()/while
  217.4 5.0 %copy-start.1 = (f32[12,2,128,128]{3,2,0,1:T(8,128)S(1)}, f32[12,2,128,128]{3,2,0,1:T(8,128)}, u32[]{:S(2)}) copy-start(f32[12,2,128,128]{3,2,0,1:T(8,128)} %copy-done) | copy-start | bytes 4718596 | tf_op jit(solution)/shard_map/vmap()/while
  235.5 5.0 %copy-start.1 = (f32[12,2,128,128]{3,2,0,1:T(8,128)S(1)}, f32[12,2,128,128]{3,2,0,1:T(8,128)}, u32[]{:S(2)}) copy-start(f32[12,2,128,128]{3,2,0,1:T(8,128)} %copy-done) | copy-start | bytes 4718596 | tf_op jit(solution)/shard_map/vmap()/while
  253.5 5.0 %copy-start.1 = (f32[12,2,128,128]{3,2,0,1:T(8,128)S(1)}, f32[12,2,128,128]{3,2,0,1:T(8,128)}, u32[]{:S(2)}) copy-start(f32[12,2,128,128]{3,2,0,1:T(8,128)} %copy-done) | copy-start | bytes 4718596 | tf_op jit(solution)/shard_map/vmap()/while
  271.6 5.0 %copy-start.1 = (f32[12,2,128,128]{3,2,0,1:T(8,128)S(1)}, f32[12,2,128,128]{3,2,0,1:T(8,128)}, u32[]{:S(2)}) copy-start(f32[12,2,128,128]{3,2,0,1:T(8,128)} %copy-done) | copy-start | bytes 4718596 | tf_op jit(solution)/shard_map/vmap()/while
  280.0 33.9 %collective-permute-start.2 = (bf16[2,1536,128]{2,1,0:T(8,128)(2,1)}, bf16[2,1536,128]{2,1,0:T(8,128)(2,1)S(1)}, u32[]{:S(2)}, u32[]{:S(2)}) collective-permute-start(bf16[2,1536,128]{2,1,0:T(8,128)(2,1)} %bitcast.74), channel_id=1, source_target_pairs={{0,124},{4,0},{8,4},{12,8},{16,12},{20,16},{24,20},{28,24},{32,28}... | collective-permute-start | bytes 2359304 | tf_op jit(solution)/shard_map/ppermute | solution.py:19
  308.9 7.5 %copy-start.5 = (bf16[2,1536,128]{2,1,0:T(8,128)(2,1)}, bf16[2,1536,128]{2,1,0:T(8,128)(2,1)S(1)}, u32[]{:S(2)}) copy-start(bf16[2,1536,128]{2,1,0:T(8,128)(2,1)S(1)} %get-tuple-element.906) | copy-start | bytes 2359300
  308.9 27.9 %collective-permute-start = (f32[2,1536,128]{2,1,0:T(8,128)}, f32[2,1536,128]{2,1,0:T(8,128)}, u32[]{:S(2)}, u32[]{:S(2)}) collective-permute-start(f32[2,1536,128]{2,1,0:T(8,128)} %bitcast.71), channel_id=1, source_target_pairs={{0,124},{4,0},{8,4},{12,8},{16,12},{20,16},{24,20},{28,24},{32,28}... | collective-permute-start | bytes 4718600 | tf_op jit(solution)/shard_map/ppermute | solution.py:19
  313.0 18.3 %collective-permute-start.9 = (f32[2,1536]{1,0:T(2,128)S(1)}, f32[2,1536]{1,0:T(2,128)S(1)}, u32[]{:S(2)}, u32[]{:S(2)}) collective-permute-start(f32[2,1536]{1,0:T(2,128)S(1)} %bitcast.530), channel_id=1, source_target_pairs={{0,124},{4,0},{8,4},{12,8},{16,12},{20,16},{24,20},{28,24},{32,28}... | collective-permute-start | bytes 36872 | tf_op jit(solution)/shard_map/ppermute | solution.py:19
  313.1 18.4 %collective-permute-start.1 = (f32[2,1536]{1,0:T(2,128)S(1)}, f32[2,1536]{1,0:T(2,128)S(1)}, u32[]{:S(2)}, u32[]{:S(2)}) collective-permute-start(f32[2,1536]{1,0:T(2,128)S(1)} %bitcast.529), channel_id=1, source_target_pairs={{0,124},{4,0},{8,4},{12,8},{16,12},{20,16},{24,20},{28,24},{32,28}... | collective-permute-start | bytes 36872 | tf_op jit(solution)/shard_map/ppermute | solution.py:19
  315.1 24.9 %collective-permute-start.5 = (bf16[2,1536,128]{2,1,0:T(8,128)(2,1)}, bf16[2,1536,128]{2,1,0:T(8,128)(2,1)}, u32[]{:S(2)}, u32[]{:S(2)}) collective-permute-start(bf16[2,1536,128]{2,1,0:T(8,128)(2,1)} %fusion.161), channel_id=1, source_target_pairs={{0,124},{4,0},{8,4},{12,8},{16,12},{20,16},{24,20},{28,24},{32,28}... | collective-permute-start | bytes 2359304 | tf_op jit(solution)/shard_map/ppermute | solution.py:19
  331.5 28.2 %collective-permute-start.10 = (f32[2,1536]{1,0:T(2,128)S(1)}, f32[2,1536]{1,0:T(2,128)S(1)}, u32[]{:S(2)}, u32[]{:S(2)}) collective-permute-start(f32[2,1536]{1,0:T(2,128)S(1)} %get-tuple-element.395), channel_id=1, source_target_pairs={{0,124},{4,0},{8,4},{12,8},{16,12},{20,16},{24,20},{28,24},{32,28}... | collective-permute-start | bytes 36872 | tf_op jit(solution)/shard_map/ppermute | solution.py:19
  336.8 23.0 %collective-permute-start.4 = (f32[2,1536]{1,0:T(2,128)S(1)}, f32[2,1536]{1,0:T(2,128)S(1)}, u32[]{:S(2)}, u32[]{:S(2)}) collective-permute-start(f32[2,1536]{1,0:T(2,128)S(1)} %get-tuple-element.449), channel_id=1, source_target_pairs={{0,124},{4,0},{8,4},{12,8},{16,12},{20,16},{24,20},{28,24},{32,28}... | collective-permute-start | bytes 36872 | tf_op jit(solution)/shard_map/ppermute | solution.py:19
  339.9 28.3 %collective-permute-start.3 = (f32[2,1536,128]{2,1,0:T(8,128)}, f32[2,1536,128]{2,1,0:T(8,128)}, u32[]{:S(2)}, u32[]{:S(2)}) collective-permute-start(f32[2,1536,128]{2,1,0:T(8,128)} %fusion.155), channel_id=1, source_target_pairs={{0,124},{4,0},{8,4},{12,8},{16,12},{20,16},{24,20},{28,24},{32,28}... | collective-permute-start | bytes 4718600 | tf_op jit(solution)/shard_map/ppermute | solution.py:19
  342.3 24.2 %collective-permute-start.8 = (bf16[2,1536,128]{2,1,0:T(8,128)(2,1)}, bf16[2,1536,128]{2,1,0:T(8,128)(2,1)}, u32[]{:S(2)}, u32[]{:S(2)}) collective-permute-start(bf16[2,1536,128]{2,1,0:T(8,128)(2,1)} %fusion.159), channel_id=1, source_target_pairs={{0,124},{4,0},{8,4},{12,8},{16,12},{20,16},{24,20},{28,24},{32,28}... | collective-permute-start | bytes 2359304 | tf_op jit(solution)/shard_map/ppermute | solution.py:19
  359.8 27.3 %collective-permute-start.11 = (f32[2,1536]{1,0:T(2,128)S(1)}, f32[2,1536]{1,0:T(2,128)S(1)}, u32[]{:S(2)}, u32[]{:S(2)}) collective-permute-start(f32[2,1536]{1,0:T(2,128)S(1)} %get-tuple-element.392), channel_id=1, source_target_pairs={{0,124},{4,0},{8,4},{12,8},{16,12},{20,16},{24,20},{28,24},{32,28}... | collective-permute-start | bytes 36872 | tf_op jit(solution)/shard_map/ppermute | solution.py:19
  359.8 27.2 %collective-permute-start.7 = (f32[2,1536]{1,0:T(2,128)S(1)}, f32[2,1536]{1,0:T(2,128)S(1)}, u32[]{:S(2)}, u32[]{:S(2)}) collective-permute-start(f32[2,1536]{1,0:T(2,128)S(1)} %get-tuple-element.448), channel_id=1, source_target_pairs={{0,124},{4,0},{8,4},{12,8},{16,12},{20,16},{24,20},{28,24},{32,28}... | collective-permute-start | bytes 36872 | tf_op jit(solution)/shard_map/ppermute | solution.py:19
  371.1 23.5 %collective-permute-start.6 = (f32[2,1536,128]{2,1,0:T(8,128)}, f32[2,1536,128]{2,1,0:T(8,128)}, u32[]{:S(2)}, u32[]{:S(2)}) collective-permute-start(f32[2,1536,128]{2,1,0:T(8,128)} %fusion.153), channel_id=1, source_target_pairs={{0,124},{4,0},{8,4},{12,8},{16,12},{20,16},{24,20},{28,24},{32,28}... | collective-permute-start | bytes 4718600 | tf_op jit(solution)/shard_map/ppermute | solution.py:19
  397.7 22.6 %collective-permute-start.12 = (bf16[2,1536,128]{2,1,0:T(8,128)(2,1)S(1)}, bf16[2,1536,128]{2,1,0:T(8,128)(2,1)S(1)}, u32[]{:S(2)}, u32[]{:S(2)}) collective-permute-start(bf16[2,1536,128]{2,1,0:T(8,128)(2,1)S(1)} %fusion.157), channel_id=1, source_target_pairs={{0,12},{4,16},{8,20},{12,24},{16,28},{20,32},{24,36},{28,40},{32,4... | collective-permute-start | bytes 2359304 | tf_op jit(solution)/shard_map/ppermute | solution.py:19
  (22 other events, 26.5 us)
where the time goes:
time: 452 us; the launch traced here: 446 us
  matrix products  180 us (40%)
  local copies, waits for them, and re-layouts  73.8 us (16%)
  other arithmetic  65.7 us (15%)
  waiting for transfers between devices  60.4 us (13%)
  starting transfers between devices  41.6 us (9%)
  blocking collectives  16.6 us (4%)
  loops' own time  6.73 us (1%)
    ppermute x13, waiting for transfers between devices, shifted(): lax.ppermute(value, axis, [(i, (i + by) % length) for i in range(length)])  40.9 us
    dot_general x24, matrix products, block_product(): results.append(vectors - jnp.dot(weights.T, normals, precision=highest))  28.4 us
    ppermute x13, starting transfers between devices, shifted(): lax.ppermute(value, axis, [(i, (i + by) % length) for i in range(length)])  23 us
    dot_general x24, matrix products, block_product(): project = jnp.dot(normals, vectors.T, precision=highest) * upper  21.7 us
    dot_general x72, matrix products, invert_upper(): jnp.matmul(first_inv, matrix[..., :half, half:], precision=highest)  21.7 us
    dot_general x72, matrix products, invert_upper(): jnp.matmul(jnp.matmul(first_inv, matrix[..., :half, half:], precision=hig...  20.8 us
    dot_general x12, matrix products, one_block(): jnp.einsum('hqk,hkd->hqd', weights.astype(jnp.bfloat16), values, preferre...  18.2 us
    dot_general x12, matrix products, one_block(): jnp.einsum('hqd,hkd->hqk', block, keys, preferred_element_type=jnp.float32)  17.1 us
  transfers between devices with their start and end apart: 17, of which 9 were waited for; matrix products, arithmetic and copies ran while one was open for 66% of the time, Pallas kernels for 0%

commit v1 on v0

v1 whole, which is shorter than its diff:
```python
import math
import jax
import jax.numpy as jnp
from jax import lax
from jax.experimental import pallas as pl
from jax.experimental.pallas import tpu as pltpu
from jax.sharding import PartitionSpec as P

DH = 128
SUB = 128
bf16 = jnp.bfloat16
f32 = jnp.float32
VMEM = pl.BlockSpec(memory_space=pltpu.VMEM)


def dot(a, b):
    return jnp.dot(a, b, preferred_element_type=f32)


def dot_t(a, b):
    return lax.dot_general(a, b, (((1,), (1,)), ((), ())), preferred_element_type=f32)


def halves(x):
    high = x.astype(bf16)
    return high, (x - high.astype(f32)).astype(bf16)


def dot3(a, b):
    return dot(
        jnp.concatenate([a[0], a[1], a[0]], axis=1), jnp.concatenate([b[0], b[0], b[1]], axis=0)
    )


def frames_kernel(w_ref, vh_ref, vl_ref, ft_ref, pt_ref, chain_ref, *, group):
    heads = w_ref.shape[1] // DH
    steps = w_ref.shape[0] // (SUB * group)
    rows = lax.broadcasted_iota(jnp.int32, (SUB, SUB), 0)
    cols = lax.broadcasted_iota(jnp.int32, (SUB, SUB), 1)
    diagonal = rows == cols
    unit = jnp.where(diagonal, 1.0, 0.0).astype(f32)
    for h in range(heads):
        chain_ref[h] = unit

    def one(step, carry):
        pairs = [(g, h) for g in range(group) for h in range(heads)]

        def at(g, h):
            start = pl.multiple_of((step * group + g) * SUB, SUB)
            return (pl.ds(start, SUB), pl.ds(h * DH, DH))

        w = [w_ref[at(*p)] for p in pairs]
        wt = [x.T for x in w]
        gram = [dot(x, t) for x, t in zip(w, wt)]
        lower, inverse = [], []
        for x in gram:
            onto = jnp.where(diagonal, x, 0.0)
            down = 2.0 / (jnp.sum(onto, axis=1, keepdims=True) + 1e-6)
            across = 2.0 / (jnp.sum(onto, axis=0, keepdims=True) + 1e-6)
            near = jnp.where((rows == cols + 1) & (rows % 2 == 1), x, 0.0)
            inverse.append(jnp.where(diagonal, down, 0.0) - near * down * across)
            lower.append(halves(x))
        size = 2
        while size < SUB:
            band = (rows // (2 * size) == cols // (2 * size)) & (rows // size > cols // size)
            split = [halves(x) for x in inverse]
            part = [
                (jnp.where(band, x[0], 0).astype(bf16), jnp.where(band, x[1], 0).astype(bf16))
                for x in lower
            ]
            half = [halves(dot3(x, y)) for x, y in zip(split, part)]
            inverse = [x - dot3(y, z) for x, y, z in zip(inverse, half, split)]
            size *= 2
        split = [halves(x) for x in inverse]
        solved = [
            halves(dot(jnp.concatenate(x, axis=1), jnp.concatenate([y, y], axis=0)))
            for x, y in zip(split, w)
        ]
        whole = [
            halves(unit - dot(jnp.concatenate([t, t], axis=1), jnp.concatenate(v, axis=0)))
            for t, v in zip(wt, solved)
        ]
        for i, p in enumerate(pairs):
            vh_ref[at(*p)] = solved[i][0]
            vl_ref[at(*p)] = solved[i][1]
        frames = [halves(chain_ref[h]) for h in range(heads)]
        for i, p in enumerate(pairs):
            h = p[1]
            ft_ref[at(*p)] = frames[h][0]
            moved = dot3(whole[i], frames[h])
            if p[0] == group - 1:
                chain_ref[h] = moved
            frames[h] = halves(moved)
        return carry

    lax.fori_loop(0, steps, one, 0)
    for h in range(heads):
        pt_ref[:, h * DH : (h + 1) * DH] = chain_ref[h].astype(bf16)


def shard_frames(w, group=2):
    rows, width = w.shape
    shape = jax.ShapeDtypeStruct((rows, width), bf16)
    return pl.pallas_call(
        lambda *refs: frames_kernel(*refs, group=group),
        out_shape=(shape, shape, shape, jax.ShapeDtypeStruct((DH, width), bf16)),
        in_specs=[VMEM],
        out_specs=(VMEM,) * 4,
        scratch_shapes=[pltpu.VMEM((width // DH, DH, DH), f32)],
        name="shard_frames",
    )(w)


def turn_kernel(x_ref, w_ref, vh_ref, vl_ref, ft_ref, pt_ref, o_ref, *, group, tail):
    length, width = x_ref.shape
    heads = width // DH
    rows = lax.broadcasted_iota(jnp.int32, (SUB, SUB), 0)
    cols = lax.broadcasted_iota(jnp.int32, (SUB, SUB), 1)
    seen = rows >= cols

    def one(step, carry):
        places = []
        for g in range(group):
            start = pl.multiple_of((step * group + g) * SUB, SUB)
            places += [(pl.ds(start, SUB), pl.ds(h * DH, DH)) for h in range(heads)]
        x = [x_ref[p] for p in places]
        onto = [halves(jnp.where(seen, dot_t(y, w_ref[p]), 0.0)) for y, p in zip(x, places)]
        turned = [
            (y.astype(f32) - dot3(z, (vh_ref[p], vl_ref[p]))).astype(bf16)
            for y, z, p in zip(x, onto, places)
        ]
        for y, p in zip(turned, places):
            o_ref[p] = dot(y, ft_ref[p]).astype(bf16)
        return carry

    lax.fori_loop(0, length // (SUB * group), one, 0)
    if tail:
        o_ref[length:, :] = pt_ref[...]


def turn(x, w, vh, vl, ft, pt, tail, group=4):
    rows, width = x.shape
    return pl.pallas_call(
        lambda *refs: turn_kernel(*refs, group=group, tail=tail),
        out_shape=jax.ShapeDtypeStruct((rows + (DH if tail else 0), width), bf16),
        in_specs=[VMEM] * 6,
        out_specs=VMEM,
        name="turn_keys" if tail else "turn_queries",
    )(x, w, vh, vl, ft, pt)

SCALE = math.log2(math.e) / math.sqrt(DH)
TILE = 256


def tile_stats(z, k, v, keep=None):
    s = dot_t(z, k)
    if keep is not None:
        s = jnp.where(keep, s, -1e30)
    best = jnp.max(s, axis=1, keepdims=True)
    p = jnp.exp2((s - best) * SCALE).astype(bf16)
    return best, dot(p, jnp.concatenate([v, jnp.ones_like(v)], axis=1))


def pack_stats(columns):
    lane = lax.broadcasted_iota(jnp.int32, (columns[0].shape[0], DH), 1)
    out = jnp.zeros(lane.shape, f32)
    for i, c in enumerate(columns):
        out = jnp.where(lane == i, c, out)
    return out


def local_kernel(q_ref, k_ref, v_ref, acc_ref, stat_ref):
    length, width = q_ref.shape
    heads = width // DH
    for i in range(length // TILE):
        size = (i + 1) * TILE
        rows = lax.broadcasted_iota(jnp.int32, (TILE, size), 0) + i * TILE
        keep = rows >= lax.broadcasted_iota(jnp.int32, (TILE, size), 1)
        columns = []
        for h in range(heads):
            lanes = slice(h * DH, (h + 1) * DH)
            best, both = tile_stats(
                q_ref[i * TILE : size, lanes], k_ref[:size, lanes], v_ref[:size, lanes], keep
            )
            acc_ref[i * TILE : size, lanes] = both[:, :DH]
            columns += [best, both[:, DH : DH + 1]]
        stat_ref[i * TILE : size, :] = pack_stats(columns)


def attend_local(zq, kp, v):
    rows, width = zq.shape
    return pl.pallas_call(
        local_kernel,
        out_shape=(
            jax.ShapeDtypeStruct((rows, width), f32),
            jax.ShapeDtypeStruct((rows, DH), f32),
        ),
        in_specs=[VMEM] * 3,
        out_specs=(VMEM,) * 2,
        name="attend_local",
    )(zq, kp, v)


def hop_kernel(ok_ref, z_ref, k_ref, v_ref, acc_ref, stat_ref, *out, last):
    length, width = z_ref.shape
    heads = width // DH
    ok = ok_ref[0] > 0

    def one(i, carry):
        rows = pl.ds(pl.multiple_of(i * TILE, TILE), TILE)
        columns = []
        for h in range(heads):
            lanes = pl.ds(h * DH, DH)
            z = dot(z_ref[rows, lanes], k_ref[length:, h * DH : (h + 1) * DH]).astype(bf16)
            best, both = tile_stats(z, k_ref[:length, h * DH : (h + 1) * DH], v_ref[:, h * DH : (h + 1) * DH])
            stat = stat_ref[rows, :]
            old = stat[:, 2 * h : 2 * h + 1]
            top = jnp.where(ok, jnp.maximum(old, best), old)
            keep = jnp.exp2((old - top) * SCALE)
            gain = jnp.where(ok, jnp.exp2((best - top) * SCALE), 0.0)
            acc = acc_ref[rows, lanes] * keep + both[:, :DH] * gain
            if last:
                total = stat[:, 2 * h + 1 : 2 * h + 2] * keep + both[:, DH:] * gain
                out[0][rows, lanes] = (acc / total).astype(bf16)
            else:
                out[0][rows, lanes] = acc
                out[2][rows, lanes] = z
                total = stat[:, 2 * h + 1 : 2 * h + 2] * keep + both[:, DH : DH + 1] * gain
                columns += [top, total]
        if not last:
            out[1][rows, :] = pack_stats(columns)
        return carry

    lax.fori_loop(0, length // TILE, one, 0)


def attend_hop(ok, z, kp, v, acc, stat, last):
    rows, width = z.shape
    small = jax.ShapeDtypeStruct((rows, width), bf16)
    shapes = (
        (small,)
        if last
        else (
            jax.ShapeDtypeStruct((rows, width), f32),
            jax.ShapeDtypeStruct((rows, DH), f32),
            small,
        )
    )
    return pl.pallas_call(
        lambda *refs: hop_kernel(*refs, last=last),
        out_shape=shapes,
        in_specs=[pl.BlockSpec(memory_space=pltpu.SMEM)] + [VMEM] * 5,
        out_specs=(VMEM,) * len(shapes),
        name="attend_last" if last else "attend_hop",
    )(ok, z, kp, v, acc, stat)


HOPS = 3


def shift(value, axis, by):
    length = lax.axis_size(axis)
    return lax.ppermute(value, axis, [(i, (i + by) % length) for i in range(length)])


def gather_heads(array):
    parts = lax.axis_size("head")
    here = lax.axis_index("head")
    rows, width = array.shape
    piece = width // parts
    out = jnp.zeros((rows * parts, piece), array.dtype)
    for k in range(parts):
        chunk = lax.dynamic_slice(array, (0, (here + k) % parts * piece), (rows, piece))
        if k:
            chunk = shift(chunk, "head", k)
        out = lax.dynamic_update_slice(out, chunk, ((here + parts - k) % parts * rows, 0))
    return out


def scatter_heads(array):
    parts = lax.axis_size("head")
    here = lax.axis_index("head")
    rows, width = array.shape
    piece = rows // parts
    out = jnp.zeros((piece, width * parts), array.dtype)
    for k in range(parts):
        chunk = lax.dynamic_slice(array, ((here + k) % parts * piece, 0), (piece, width))
        if k:
            chunk = shift(chunk, "head", k)
        out = lax.dynamic_update_slice(out, chunk, (0, (here + parts - k) % parts * width))
    return out


def body(queries, keys, values, directions):
    v = gather_heads(values)
    w = gather_heads(directions)
    k = gather_heads(keys)
    q = gather_heads(queries)
    vh, vl, ft, pt = shard_frames(w, 4)
    kp = turn(k, w, vh, vl, ft, pt, True)
    z = turn(q, w, vh, vl, ft, pt, False)
    acc, stat = attend_local(z, kp, v)
    position = lax.axis_index("ctx")
    for distance in range(1, HOPS + 1):
        v = shift(v, "ctx", 1)
        kp = shift(kp, "ctx", 1)
        ok = (position >= distance).astype(jnp.int32).reshape(1)
        out = attend_hop(ok, z, kp, v, acc, stat, distance == HOPS)
        if distance < HOPS:
            acc, stat, z = out
    return scatter_heads(out[0])


def solution(mesh):
    spec = P(("ctx", "head"), None)
    return jax.shard_map(
        body, mesh=mesh, in_specs=(spec,) * 4, out_specs=spec, check_vma=False
    )
```

time: 452 us -> 180 us (0.40); the launches traced: 446 us -> 179 us
  matrix products: 180 us -> 0 us
  Pallas kernels: 0 us -> 75.5 us
  other arithmetic: 65.7 us -> 0 us
  local copies, waits for them, and re-layouts: 73.8 us -> 17.3 us
  starting transfers between devices: 41.6 us -> 24.1 us
  blocking collectives: 16.6 us -> 0 us
  loops' own time: 6.73 us -> 0 us
    dot_general x315 -> x0, matrix products: 180 us -> none  [the longest x24 28.4 us: block_product(): results.append(vectors - jnp.dot(weights.T, normals, precision=highest))]
    pallas_call x0 -> x7, Pallas kernels: none -> 75.5 us  [the longest x3 44.2 us: attend_hop(): pl.pallas_call(lambda *refs: hop_kernel(*refs, last=last), out_shape=shap...]
    transpose x29 -> x0, local copies, waits for them, and re-layouts: 22.1 us -> none  [the longest x4 8.05 us: shard_frames(): lax.scan(advance, jnp.eye(width, dtype=jnp.float32), (normals, query_bloc...]
    ppermute x13 -> x21, waiting for transfers between devices: 40.9 us -> 62 us  [shift(): lax.ppermute(value, axis, [(i, (i + by) % length) for i in range(length)])]
    all_to_all x4 -> x0, waiting for transfers between devices: 19.5 us -> none  [the longest x1 9.42 us: body(): lax.all_to_all(directions, 'head', split_axis=1, concat_axis=0, tiled=True)]
    reduce_sum x13 -> x0, other arithmetic: 19.2 us -> none  [the longest x12 16.6 us: one_block(): total = jnp.sum(weights, axis=-1)]
    all_to_all x4 -> x0, starting transfers between devices: 18.6 us -> none  [the longest x1 5.55 us: body(): lax.all_to_all(directions, 'head', split_axis=1, concat_axis=0, tiled=True)]
    all_to_all x1 -> x0, blocking collectives: 16.6 us -> none  [body(): lax.all_to_all(merged, 'head', split_axis=0, concat_axis=1, tiled=True)]
  transfers between devices with their start and end apart: 17 -> 21, of which waited for: 9 -> 8; matrix products, arithmetic and copies ran while one was open for 66% -> 5% of each run, Pallas kernels for 0% -> 35%
where the time goes in v1:
time: 180 us; the launch traced here: 179 us
  Pallas kernels  75.5 us (42%)
  waiting for transfers between devices  62 us (34%)
  starting transfers between devices  24.1 us (13%)
  local copies, waits for them, and re-layouts  17.3 us (10%)
    ppermute x21, waiting for transfers between devices, shift(): lax.ppermute(value, axis, [(i, (i + by) % length) for i in range(length)])  62 us
    pallas_call x3, Pallas kernels, attend_hop(): pl.pallas_call(lambda *refs: hop_kernel(*refs, last=last), out_shape=shap...  44.2 us
    ppermute x21, starting transfers between devices, shift(): lax.ppermute(value, axis, [(i, (i + by) % length) for i in range(length)])  24.1 us
    pallas_call x1, Pallas kernels, shard_frames(): pl.pallas_call(lambda *refs: frames_kernel(*refs, group=group), out_shape...  13.6 us
    pallas_call x2, Pallas kernels, turn(): pl.pallas_call(lambda *refs: turn_kernel(*refs, group=group, tail=tail),...  9.91 us
    pallas_call x1, Pallas kernels, attend_local(): pl.pallas_call(local_kernel, out_shape=(jax.ShapeDtypeStruct((rows, width...  7.75 us
    dynamic_update_slice x12, local copies, waits for them, and re-layouts, gather_heads(): lax.dynamic_update_slice(out, chunk, ((here + parts - k) % parts * rows, 0))  6.77 us
    dynamic_slice x4, local copies, waits for them, and re-layouts, gather_heads(): lax.dynamic_slice(array, (0, (here + k) % parts * piece), (rows, piece))  4.72 us
  transfers between devices with their start and end apart: 21, of which 8 were waited for; matrix products, arithmetic and copies ran while one was open for 5% of the time, Pallas kernels for 35%

profile of v1, /device:TPU:0, one launch (start us, length us, event | category | flops | bytes accessed | tf_op | source)
XLA Modules:
  0.0 179.3 jit_solution(12492037570534643264)
XLA Ops:
  0.1 2.1 %constant_dynamic-slice_fusion.8 = (bf16[384,256]{1,0:T(8,128)(2,1)}, bf16[384,256]{1,0:T(8,128)(2,1)}, bf16[1536,256]{1,0:T(8,128)(2,1)S(1)}, bf16[384,256]{1,0:T(8,128)(2,1)}) fusion(bf16[384,1024]{1,0:T(8,128)(2,1)} %param.7, s32[]{:T(128)S(6)} %select_n.164, s32[]{:T(128)S(6)} %select_n.158, bf16[1536,256]{1,0:T(8,128)(2,1)S(1)} %broadcast.11.clone.1, ...), kind=kLoop, calls=%fused_computation.22 | loop fusion | bytes 1572884 | tf_op jit(solution)/shard_map/dynamic_slice | solution.py:273
  2.2 2.0 %collective-permute-start.3 = (bf16[384,256]{1,0:T(8,128)(2,1)}, bf16[384,256]{1,0:T(8,128)(2,1)}, u32[]{:S(2)}, u32[]{:S(2)}) collective-permute-start(bf16[384,256]{1,0:T(8,128)(2,1)} %get-tuple-element.42), channel_id=1, source_target_pairs={{0,1},{1,2},{2,3},{3,0},{4,5},{5,6},{6,7},{7,4},{8,9},{9,10},{10,1... | collective-permute-start | bytes 589832 | tf_op jit(solution)/shard_map/ppermute | solution.py:263
  5.1 1.9 %collective-permute-start.6 = (bf16[384,256]{1,0:T(8,128)(2,1)}, bf16[384,256]{1,0:T(8,128)(2,1)}, u32[]{:S(2)}, u32[]{:S(2)}) collective-permute-start(bf16[384,256]{1,0:T(8,128)(2,1)} %get-tuple-element.38), channel_id=1, source_target_pairs={{0,1},{1,2},{2,3},{3,0},{4,5},{5,6},{6,7},{7,4},{8,9},{9,10},{10,1... | collective-permute-start | bytes 589832 | tf_op jit(solution)/shard_map/ppermute | solution.py:263
  7.1 1.7 collective-permute-start.7
  8.7 2.6 %collective-permute-start.8 = (bf16[384,256]{1,0:T(8,128)(2,1)}, bf16[384,256]{1,0:T(8,128)(2,1)S(1)}, u32[]{:S(2)}, u32[]{:S(2)}) collective-permute-start(bf16[384,256]{1,0:T(8,128)(2,1)} %get-tuple-element.37), channel_id=1, source_target_pairs={{0,3},{1,0},{2,1},{3,2},{4,7},{5,4},{6,5},{7,6},{8,11},{9,8},{10,9... | collective-permute-start | bytes 589832 | tf_op jit(solution)/shard_map/ppermute | solution.py:263
  12.4 2.0 %collective-permute-start.5 = (bf16[384,256]{1,0:T(8,128)(2,1)}, bf16[384,256]{1,0:T(8,128)(2,1)S(1)}, u32[]{:S(2)}, u32[]{:S(2)}) collective-permute-start(bf16[384,256]{1,0:T(8,128)(2,1)} %get-tuple-element.41), channel_id=1, source_target_pairs={{0,3},{1,0},{2,1},{3,2},{4,7},{5,4},{6,5},{7,6},{8,11},{9,8},{10,9... | collective-permute-start | bytes 589832 | tf_op jit(solution)/shard_map/ppermute | solution.py:263
  15.3 10.0 %collective-permute-done.4 = bf16[384,256]{1,0:T(8,128)(2,1)} collective-permute-done((bf16[384,256]{1,0:T(8,128)(2,1)}, bf16[384,256]{1,0:T(8,128)(2,1)}, u32[]{:S(2)}, u32[]{:S(2)}) %collective-permute-start.4) | collective-permute-done | bytes 196640 | tf_op jit(solution)/shard_map/ppermute | solution.py:263
  25.4 1.4 collective-permute-start.10
  27.7 2.1 %collective-permute-start.11 = (bf16[384,256]{1,0:T(8,128)(2,1)}, bf16[384,256]{1,0:T(8,128)(2,1)}, u32[]{:S(2)}, u32[]{:S(2)}) collective-permute-start(bf16[384,256]{1,0:T(8,128)(2,1)} %get-tuple-element.36), channel_id=1, source_target_pairs={{0,2},{1,3},{2,0},{3,1},{4,6},{5,7},{6,4},{7,5},{8,10},{9,11},{10,... | collective-permute-start | bytes 589832 | tf_op jit(solution)/shard_map/ppermute | solution.py:263
  30.7 13.6 %shard_frames.1 = (bf16[1536,256]{1,0:T(8,128)(2,1)}, bf16[1536,256]{1,0:T(8,128)(2,1)}, bf16[1536,256]{1,0:T(8,128)(2,1)}, bf16[128,256]{1,0:T(8,128)(2,1)}) custom-call(bf16[1536,256]{1,0:T(8,128)(2,1)} %copy-done), custom_call_target="tpu_custom_call" | custom-call | tf_op jit(solution)/shard_map/shard_frames/pallas_call | solution.py:104
  47.0 5.0 %turn_keys.1.k_ref = bf16[1664,256]{1,0:T(8,128)(2,1)} custom-call(bf16[1536,256]{1,0:T(8,128)(2,1)} %copy-done.2, bf16[1536,256]{1,0:T(8,128)(2,1)} %copy-done, bf16[1536,256]{1,0:T(8,128)(2,1)} %get-tuple-element.17.refs_2_, bf16[1536,256]{1,0:T(8,128)(2,1)} %get-tuple-element.18.refs_3_, bf16[1536,256]{1,0:T(8,128)(2,1)} %get-tuple-element.19.refs_4_, ...), custom_call_target="tpu_custom_call" | custom-call | tf_op jit(solution)/shard_map/turn_keys/pallas_call | solution.py:143
  52.0 1.0 constant_dynamic-update-slice_fusion.3
  53.0 0.9 constant_dynamic-update-slice_fusion.2
  54.0 1.7 collective-permute-start.13
  55.7 11.9 %collective-permute-done.9.refs_2_ = bf16[1664,256]{1,0:T(8,128)(2,1)S(1)} collective-permute-done((bf16[1664,256]{1,0:T(8,128)(2,1)}, bf16[1664,256]{1,0:T(8,128)(2,1)S(1)}, u32[]{:S(2)}, u32[]{:S(2)}) %collective-permute-start.9) | collective-permute-done | bytes 852000 | tf_op jit(solution)/shard_map/ppermute | solution.py:263
  67.6 8.4 %collective-permute-done.13.refs_3_ = bf16[1536,256]{1,0:T(8,128)(2,1)S(1)} collective-permute-done((bf16[1536,256]{1,0:T(8,128)(2,1)S(1)}, bf16[1536,256]{1,0:T(8,128)(2,1)S(1)}, u32[]{:S(2)}, u32[]{:S(2)}) %collective-permute-start.13) | collective-permute-done | bytes 786464 | tf_op jit(solution)/shard_map/ppermute | solution.py:263
  76.0 9.2 %collective-permute-done.14.refs_2_ = bf16[1664,256]{1,0:T(8,128)(2,1)} collective-permute-done((bf16[1664,256]{1,0:T(8,128)(2,1)S(1)}, bf16[1664,256]{1,0:T(8,128)(2,1)}, u32[]{:S(2)}, u32[]{:S(2)}) %collective-permute-start.14) | collective-permute-done | bytes 852000 | tf_op jit(solution)/shard_map/ppermute | solution.py:263
  85.3 8.4 %collective-permute-done.15.refs_3_ = bf16[1536,256]{1,0:T(8,128)(2,1)} collective-permute-done((bf16[1536,256]{1,0:T(8,128)(2,1)S(1)}, bf16[1536,256]{1,0:T(8,128)(2,1)}, u32[]{:S(2)}, u32[]{:S(2)}) %collective-permute-start.15) | collective-permute-done | bytes 786464 | tf_op jit(solution)/shard_map/ppermute | solution.py:263
  94.6 1.2 collective-permute-start
  95.9 1.5 collective-permute-start.1
  97.4 1.9 %collective-permute-start.2 = (bf16[384,256]{1,0:T(8,128)(2,1)}, bf16[384,256]{1,0:T(8,128)(2,1)S(1)}, u32[]{:S(2)}, u32[]{:S(2)}) collective-permute-start(bf16[384,256]{1,0:T(8,128)(2,1)} %get-tuple-element.45), channel_id=1, source_target_pairs={{0,3},{1,0},{2,1},{3,2},{4,7},{5,4},{6,5},{7,6},{8,11},{9,8},{10,9... | collective-permute-start | bytes 589832 | tf_op jit(solution)/shard_map/ppermute | solution.py:263
  99.3 6.3 %collective-permute-done = bf16[384,256]{1,0:T(8,128)(2,1)} collective-permute-done((bf16[384,256]{1,0:T(8,128)(2,1)}, bf16[384,256]{1,0:T(8,128)(2,1)}, u32[]{:S(2)}, u32[]{:S(2)}) %collective-permute-start) | collective-permute-done | bytes 196640 | tf_op jit(solution)/shard_map/ppermute | solution.py:263
  105.6 0.9 constant_dynamic-update-slice_fusion.13
  106.5 0.9 constant_dynamic-update-slice_fusion.12
  108.4 4.9 %turn_queries.1.q_ref.refs_1_ = bf16[1536,256]{1,0:T(8,128)(2,1)} custom-call(bf16[1536,256]{1,0:T(8,128)(2,1)} %copy-done.1, bf16[1536,256]{1,0:T(8,128)(2,1)} %copy-done, bf16[1536,256]{1,0:T(8,128)(2,1)} %get-tuple-element.17.refs_2_, bf16[1536,256]{1,0:T(8,128)(2,1)} %get-tuple-element.18.refs_3_, bf16[1536,256]{1,0:T(8,128)(2,1)} %get-tuple-element.19.refs_4_, ...), custom_call_target="tpu_custom_call" | custom-call | tf_op jit(solution)/shard_map/turn_queries/pallas_call | solution.py:143
  113.3 7.7 %attend_local.1 = (f32[1536,256]{1,0:T(8,128)}, f32[1536,128]{1,0:T(8,128)}) custom-call(bf16[1536,256]{1,0:T(8,128)(2,1)} %turn_queries.1.q_ref.refs_1_, bf16[1664,256]{1,0:T(8,128)(2,1)} %turn_keys.1.k_ref, bf16[1536,256]{1,0:T(8,128)(2,1)} %copy-done.3), custom_call_target="tpu_custom_call" | custom-call | tf_op jit(solution)/shard_map/attend_local/pallas_call | solution.py:192
  121.1 15.3 %attend_hop.2 = (f32[1536,256]{1,0:T(8,128)}, f32[1536,128]{1,0:T(8,128)}, bf16[1536,256]{1,0:T(8,128)(2,1)}) custom-call(s32[1]{0:T(128)} %bitcast.2.refs_0_, bf16[1536,256]{1,0:T(8,128)(2,1)} %turn_queries.1.q_ref.refs_1_, bf16[1664,256]{1,0:T(8,128)(2,1)} %copy-done.4, bf16[1536,256]{1,0:T(8,128)(2,1)} %copy-done.5, ...), custom_call_target="tpu_custom_call" | custom-call | tf_op jit(solution)/shard_map/attend_hop/pallas_call | solution.py:249
  136.4 15.3 %attend_hop.3 = (f32[1536,256]{1,0:T(8,128)}, f32[1536,128]{1,0:T(8,128)}, bf16[1536,256]{1,0:T(8,128)(2,1)}) custom-call(s32[1]{0:T(128)} %bitcast.1.refs_0_, bf16[1536,256]{1,0:T(8,128)(2,1)} %get-tuple-element.23.refs_1_, bf16[1664,256]{1,0:T(8,128)(2,1)} %collective-permute-done.14.refs_2_, bf16[1536,256]{1,0:T(8,128)(2,1)} %collective-permute-done.15.refs_3_, ...), custom_call_target="tpu_custom_call" | custom-call | tf_op jit(solution)/shard_map/attend_hop/pallas_call | solution.py:249
  151.8 13.6 %attend_last.1 = bf16[1536,256]{1,0:T(8,128)(2,1)} custom-call(s32[1]{0:T(128)} %bitcast.refs_0_, bf16[1536,256]{1,0:T(8,128)(2,1)} %get-tuple-element.26.refs_1_, bf16[1664,256]{1,0:T(8,128)(2,1)} %collective-permute-done.16.refs_2_, bf16[1536,256]{1,0:T(8,128)(2,1)} %collective-permute-done.17.refs_3_, f32[1536,256]{1,0:T(8,128)} %get-tuple-element.27.refs_4_, ...), custom_call_target="tpu_custom_call" | custom-call | tf_op jit(solution)/shard_map/attend_last/pallas_call | solution.py:249
  165.4 1.3 constant_dynamic-slice_fusion.4
  166.8 2.6 %collective-permute-start.19 = (bf16[384,256]{1,0:T(8,128)(2,1)S(1)}, bf16[384,256]{1,0:T(8,128)(2,1)S(1)}, u32[]{:S(2)}, u32[]{:S(2)}) collective-permute-start(bf16[384,256]{1,0:T(8,128)(2,1)S(1)} %get-tuple-element.30), channel_id=1, source_target_pairs={{0,2},{1,3},{2,0},{3,1},{4,6},{5,7},{6,4},{7,5},{8,10},{9,11},{10,... | collective-permute-start | bytes 589832 | tf_op jit(solution)/shard_map/ppermute | solution.py:263
  170.0 7.6 %collective-permute-done.18 = bf16[384,256]{1,0:T(8,128)(2,1)S(1)} collective-permute-done((bf16[384,256]{1,0:T(8,128)(2,1)S(1)}, bf16[384,256]{1,0:T(8,128)(2,1)S(1)}, u32[]{:S(2)}, u32[]{:S(2)}) %collective-permute-start.18) | collective-permute-done | bytes 196640 | tf_op jit(solution)/shard_map/ppermute | solution.py:263
  (62 shorter events, 11.7 us)
Async XLA Ops:
  0.0 4.3 %copy-start.6 = (bf16[384,1024]{1,0:T(8,128)(2,1)S(1)}, bf16[384,1024]{1,0:T(8,128)(2,1)}, u32[]{:S(2)}) copy-start(bf16[384,1024]{1,0:T(8,128)(2,1)} %param.5) | copy-start | bytes 2359300
  2.2 9.3 %copy-start.7 = (bf16[384,1024]{1,0:T(8,128)(2,1)S(1)}, bf16[384,1024]{1,0:T(8,128)(2,1)}, u32[]{:S(2)}) copy-start(bf16[384,1024]{1,0:T(8,128)(2,1)} %param.6) | copy-start | bytes 2359300
  2.2 10.2 %collective-permute-start.3 = (bf16[384,256]{1,0:T(8,128)(2,1)}, bf16[384,256]{1,0:T(8,128)(2,1)}, u32[]{:S(2)}, u32[]{:S(2)}) collective-permute-start(bf16[384,256]{1,0:T(8,128)(2,1)} %get-tuple-element.42), channel_id=1, source_target_pairs={{0,1},{1,2},{2,3},{3,0},{4,5},{5,6},{6,7},{7,4},{8,9},{9,10},{10,1... | collective-permute-start | bytes 589832 | tf_op jit(solution)/shard_map/ppermute | solution.py:263
  5.1 39.2 %collective-permute-start.6 = (bf16[384,256]{1,0:T(8,128)(2,1)}, bf16[384,256]{1,0:T(8,128)(2,1)}, u32[]{:S(2)}, u32[]{:S(2)}) collective-permute-start(bf16[384,256]{1,0:T(8,128)(2,1)} %get-tuple-element.38), channel_id=1, source_target_pairs={{0,1},{1,2},{2,3},{3,0},{4,5},{5,6},{6,7},{7,4},{8,9},{9,10},{10,1... | collective-permute-start | bytes 589832 | tf_op jit(solution)/shard_map/ppermute | solution.py:263
  7.1 39.0 %collective-permute-start.7 = (bf16[384,256]{1,0:T(8,128)(2,1)}, bf16[384,256]{1,0:T(8,128)(2,1)S(1)}, u32[]{:S(2)}, u32[]{:S(2)}) collective-permute-start(bf16[384,256]{1,0:T(8,128)(2,1)} %get-tuple-element.40), channel_id=1, source_target_pairs={{0,2},{1,3},{2,0},{3,1},{4,6},{5,7},{6,4},{7,5},{8,10},{9,11},{10,... | collective-permute-start | bytes 589832 | tf_op jit(solution)/shard_map/ppermute | solution.py:263
  8.7 37.3 %collective-permute-start.8 = (bf16[384,256]{1,0:T(8,128)(2,1)}, bf16[384,256]{1,0:T(8,128)(2,1)S(1)}, u32[]{:S(2)}, u32[]{:S(2)}) collective-permute-start(bf16[384,256]{1,0:T(8,128)(2,1)} %get-tuple-element.37), channel_id=1, source_target_pairs={{0,3},{1,0},{2,1},{3,2},{4,7},{5,4},{6,5},{7,6},{8,11},{9,8},{10,9... | collective-permute-start | bytes 589832 | tf_op jit(solution)/shard_map/ppermute | solution.py:263
  11.4 14.0 %collective-permute-start.4 = (bf16[384,256]{1,0:T(8,128)(2,1)}, bf16[384,256]{1,0:T(8,128)(2,1)}, u32[]{:S(2)}, u32[]{:S(2)}) collective-permute-start(bf16[384,256]{1,0:T(8,128)(2,1)} %get-tuple-element.44), channel_id=1, source_target_pairs={{0,2},{1,3},{2,0},{3,1},{4,6},{5,7},{6,4},{7,5},{8,10},{9,11},{10,... | collective-permute-start | bytes 589832 | tf_op jit(solution)/shard_map/ppermute | solution.py:263
  12.4 15.3 %collective-permute-start.5 = (bf16[384,256]{1,0:T(8,128)(2,1)}, bf16[384,256]{1,0:T(8,128)(2,1)S(1)}, u32[]{:S(2)}, u32[]{:S(2)}) collective-permute-start(bf16[384,256]{1,0:T(8,128)(2,1)} %get-tuple-element.41), channel_id=1, source_target_pairs={{0,3},{1,0},{2,1},{3,2},{4,7},{5,4},{6,5},{7,6},{8,11},{9,8},{10,9... | collective-permute-start | bytes 589832 | tf_op jit(solution)/shard_map/ppermute | solution.py:263
  25.4 26.6 %collective-permute-start.10 = (bf16[384,256]{1,0:T(8,128)(2,1)}, bf16[384,256]{1,0:T(8,128)(2,1)}, u32[]{:S(2)}, u32[]{:S(2)}) collective-permute-start(bf16[384,256]{1,0:T(8,128)(2,1)} %get-tuple-element.34), channel_id=1, source_target_pairs={{0,1},{1,2},{2,3},{3,0},{4,5},{5,6},{6,7},{7,4},{8,9},{9,10},{10,1... | collective-permute-start | bytes 589832 | tf_op jit(solution)/shard_map/ppermute | solution.py:263
  27.7 25.3 %collective-permute-start.11 = (bf16[384,256]{1,0:T(8,128)(2,1)}, bf16[384,256]{1,0:T(8,128)(2,1)}, u32[]{:S(2)}, u32[]{:S(2)}) collective-permute-start(bf16[384,256]{1,0:T(8,128)(2,1)} %get-tuple-element.36), channel_id=1, source_target_pairs={{0,2},{1,3},{2,0},{3,1},{4,6},{5,7},{6,4},{7,5},{8,10},{9,11},{10,... | collective-permute-start | bytes 589832 | tf_op jit(solution)/shard_map/ppermute | solution.py:263
  29.8 0.9 copy-start
  44.3 9.7 %collective-permute-start.12 = (bf16[384,256]{1,0:T(8,128)(2,1)}, bf16[384,256]{1,0:T(8,128)(2,1)S(1)}, u32[]{:S(2)}, u32[]{:S(2)}) collective-permute-start(bf16[384,256]{1,0:T(8,128)(2,1)} %get-tuple-element.33), channel_id=1, source_target_pairs={{0,3},{1,0},{2,1},{3,2},{4,7},{5,4},{6,5},{7,6},{8,11},{9,8},{10,9... | collective-permute-start | bytes 589832 | tf_op jit(solution)/shard_map/ppermute | solution.py:263
  46.1 0.9 copy-start.2
  52.0 41.8 %copy-start.8 = (bf16[384,1024]{1,0:T(8,128)(2,1)S(1)}, bf16[384,1024]{1,0:T(8,128)(2,1)}, u32[]{:S(2)}) copy-start(bf16[384,1024]{1,0:T(8,128)(2,1)} %param.4) | copy-start | bytes 2359300
  52.0 15.6 %collective-permute-start.9 = (bf16[1664,256]{1,0:T(8,128)(2,1)}, bf16[1664,256]{1,0:T(8,128)(2,1)S(1)}, u32[]{:S(2)}, u32[]{:S(2)}) collective-permute-start(bf16[1664,256]{1,0:T(8,128)(2,1)} %turn_keys.1.k_ref), channel_id=1, source_target_pairs={{0,4},{4,8},{8,12},{12,16},{16,20},{20,24},{24,28},{28,32},{32,36}... | collective-permute-start | bytes 2555912 | tf_op jit(solution)/shard_map/ppermute | solution.py:263
  54.0 53.5 %copy-start.3 = (bf16[1536,256]{1,0:T(8,128)(2,1)}, bf16[1536,256]{1,0:T(8,128)(2,1)S(1)}, u32[]{:S(2)}) copy-start(bf16[1536,256]{1,0:T(8,128)(2,1)S(1)} %constant_dynamic-update-slice_fusion.1.v_ref) | copy-start | bytes 2359300
  54.0 22.0 %collective-permute-start.13 = (bf16[1536,256]{1,0:T(8,128)(2,1)S(1)}, bf16[1536,256]{1,0:T(8,128)(2,1)S(1)}, u32[]{:S(2)}, u32[]{:S(2)}) collective-permute-start(bf16[1536,256]{1,0:T(8,128)(2,1)S(1)} %constant_dynamic-update-slice_fusion.1.v_ref), channel_id=1, source_target_pairs={{0,4},{4,8},{8,12},{12,16},{16,20},{20,24},{24,28},{28,32},{32,36}... | collective-permute-start | bytes 2359304 | tf_op jit(solution)/shard_map/ppermute | solution.py:263
  67.6 39.9 %copy-start.4 = (bf16[1664,256]{1,0:T(8,128)(2,1)}, bf16[1664,256]{1,0:T(8,128)(2,1)S(1)}, u32[]{:S(2)}) copy-start(bf16[1664,256]{1,0:T(8,128)(2,1)S(1)} %collective-permute-done.9.refs_2_) | copy-start | bytes 2555908
  67.6 17.7 %collective-permute-start.14 = (bf16[1664,256]{1,0:T(8,128)(2,1)S(1)}, bf16[1664,256]{1,0:T(8,128)(2,1)}, u32[]{:S(2)}, u32[]{:S(2)}) collective-permute-start(bf16[1664,256]{1,0:T(8,128)(2,1)S(1)} %collective-permute-done.9.refs_2_), channel_id=1, source_target_pairs={{0,4},{4,8},{8,12},{12,16},{16,20},{20,24},{24,28},{28,32},{32,36}... | collective-permute-start | bytes 2555912 | tf_op jit(solution)/shard_map/ppermute | solution.py:263
  76.0 31.4 %copy-start.5 = (bf16[1536,256]{1,0:T(8,128)(2,1)}, bf16[1536,256]{1,0:T(8,128)(2,1)S(1)}, u32[]{:S(2)}) copy-start(bf16[1536,256]{1,0:T(8,128)(2,1)S(1)} %collective-permute-done.13.refs_3_) | copy-start | bytes 2359300
  76.0 17.7 %collective-permute-start.15 = (bf16[1536,256]{1,0:T(8,128)(2,1)S(1)}, bf16[1536,256]{1,0:T(8,128)(2,1)}, u32[]{:S(2)}, u32[]{:S(2)}) collective-permute-start(bf16[1536,256]{1,0:T(8,128)(2,1)S(1)} %collective-permute-done.13.refs_3_), channel_id=1, source_target_pairs={{0,4},{4,8},{8,12},{12,16},{16,20},{20,24},{24,28},{28,32},{32,36}... | collective-permute-start | bytes 2359304 | tf_op jit(solution)/shard_map/ppermute | solution.py:263
  85.3 66.5 %collective-permute-start.16 = (bf16[1664,256]{1,0:T(8,128)(2,1)}, bf16[1664,256]{1,0:T(8,128)(2,1)}, u32[]{:S(2)}, u32[]{:S(2)}) collective-permute-start(bf16[1664,256]{1,0:T(8,128)(2,1)} %collective-permute-done.14.refs_2_), channel_id=1, source_target_pairs={{0,4},{4,8},{8,12},{12,16},{16,20},{20,24},{24,28},{28,32},{32,36}... | collective-permute-start | bytes 2555912 | tf_op jit(solution)/shard_map/ppermute | solution.py:263
  93.7 58.1 %collective-permute-start.17 = (bf16[1536,256]{1,0:T(8,128)(2,1)}, bf16[1536,256]{1,0:T(8,128)(2,1)}, u32[]{:S(2)}, u32[]{:S(2)}) collective-permute-start(bf16[1536,256]{1,0:T(8,128)(2,1)} %collective-permute-done.15.refs_3_), channel_id=1, source_target_pairs={{0,4},{4,8},{8,12},{12,16},{16,20},{20,24},{24,28},{28,32},{32,36}... | collective-permute-start | bytes 2359304 | tf_op jit(solution)/shard_map/ppermute | solution.py:263
  94.6 10.9 %collective-permute-start = (bf16[384,256]{1,0:T(8,128)(2,1)}, bf16[384,256]{1,0:T(8,128)(2,1)}, u32[]{:S(2)}, u32[]{:S(2)}) collective-permute-start(bf16[384,256]{1,0:T(8,128)(2,1)} %get-tuple-element.46), channel_id=1, source_target_pairs={{0,1},{1,2},{2,3},{3,0},{4,5},{5,6},{6,7},{7,4},{8,9},{9,10},{10,1... | collective-permute-start | bytes 589832 | tf_op jit(solution)/shard_map/ppermute | solution.py:263
  95.9 10.6 %collective-permute-start.1 = (bf16[384,256]{1,0:T(8,128)(2,1)}, bf16[384,256]{1,0:T(8,128)(2,1)}, u32[]{:S(2)}, u32[]{:S(2)}) collective-permute-start(bf16[384,256]{1,0:T(8,128)(2,1)} %get-tuple-element.48), channel_id=1, source_target_pairs={{0,2},{1,3},{2,0},{3,1},{4,6},{5,7},{6,4},{7,5},{8,10},{9,11},{10,... | collective-permute-start | bytes 589832 | tf_op jit(solution)/shard_map/ppermute | solution.py:263
  97.4 10.1 %collective-permute-start.2 = (bf16[384,256]{1,0:T(8,128)(2,1)}, bf16[384,256]{1,0:T(8,128)(2,1)S(1)}, u32[]{:S(2)}, u32[]{:S(2)}) collective-permute-start(bf16[384,256]{1,0:T(8,128)(2,1)} %get-tuple-element.45), channel_id=1, source_target_pairs={{0,3},{1,0},{2,1},{3,2},{4,7},{5,4},{6,5},{7,6},{8,11},{9,8},{10,9... | collective-permute-start | bytes 589832 | tf_op jit(solution)/shard_map/ppermute | solution.py:263
  107.5 0.9 copy-start.1
  166.7 10.9 %collective-permute-start.18 = (bf16[384,256]{1,0:T(8,128)(2,1)S(1)}, bf16[384,256]{1,0:T(8,128)(2,1)S(1)}, u32[]{:S(2)}, u32[]{:S(2)}) collective-permute-start(bf16[384,256]{1,0:T(8,128)(2,1)S(1)} %get-tuple-element.31), channel_id=1, source_target_pairs={{0,1},{1,2},{2,3},{3,0},{4,5},{5,6},{6,7},{7,4},{8,9},{9,10},{10,1... | collective-permute-start | bytes 589832 | tf_op jit(solution)/shard_map/ppermute | solution.py:263
  166.8 10.8 %collective-permute-start.19 = (bf16[384,256]{1,0:T(8,128)(2,1)S(1)}, bf16[384,256]{1,0:T(8,128)(2,1)S(1)}, u32[]{:S(2)}, u32[]{:S(2)}) collective-permute-start(bf16[384,256]{1,0:T(8,128)(2,1)S(1)} %get-tuple-element.30), channel_id=1, source_target_pairs={{0,2},{1,3},{2,0},{3,1},{4,6},{5,7},{6,4},{7,5},{8,10},{9,11},{10,... | collective-permute-start | bytes 589832 | tf_op jit(solution)/shard_map/ppermute | solution.py:263
  169.4 8.3 %collective-permute-start.20 = (bf16[384,256]{1,0:T(8,128)(2,1)S(1)}, bf16[384,256]{1,0:T(8,128)(2,1)S(1)}, u32[]{:S(2)}, u32[]{:S(2)}) collective-permute-start(bf16[384,256]{1,0:T(8,128)(2,1)S(1)} %get-tuple-element.29), channel_id=1, source_target_pairs={{0,3},{1,0},{2,1},{3,2},{4,7},{5,4},{6,5},{7,6},{8,11},{9,8},{10,9... | collective-permute-start | bytes 589832 | tf_op jit(solution)/shard_map/ppermute | solution.py:263
  177.7 0.9 copy-start.9

commit v2 on v1

v2 whole, which is shorter than its diff:
```python
import math
import jax
import jax.numpy as jnp
from jax import lax
from jax.experimental import pallas as pl
from jax.experimental.pallas import tpu as pltpu
from jax.sharding import PartitionSpec as P

DH = 128
SUB = 128
bf16 = jnp.bfloat16
f32 = jnp.float32
VMEM = pl.BlockSpec(memory_space=pltpu.VMEM)
SMEM = pl.BlockSpec(memory_space=pltpu.SMEM)
GRANT = 24 << 20
COST = 10**8


near = pltpu.VMEM


def keep_near(x):
    return pltpu.with_memory_space_constraint(x, pltpu.VMEM)


def dot(a, b):
    return jnp.dot(a, b, preferred_element_type=f32)


def dot_t(a, b):
    return lax.dot_general(a, b, (((1,), (1,)), ((), ())), preferred_element_type=f32)


def halves(x):
    high = x.astype(bf16)
    return high, (x - high.astype(f32)).astype(bf16)


def thirds(x):
    high = x.astype(bf16)
    rest = x - high.astype(f32)
    middle = rest.astype(bf16)
    return high, middle, (rest - middle.astype(f32)).astype(bf16)


def dot6(a, b):
    return dot(
        jnp.concatenate([a[0], a[1], a[2], a[0], a[1], a[0]], axis=1),
        jnp.concatenate([b[0], b[0], b[0], b[1], b[1], b[2]], axis=0),
    )


def dot3(a, b):
    return dot(
        jnp.concatenate([a[0], a[1], a[0]], axis=1), jnp.concatenate([b[0], b[0], b[1]], axis=0)
    )


def put_chunks(here_ref, chunks, out_ref):
    here = here_ref[0]
    parts = len(chunks)
    rows = chunks[0].shape[0]
    for k, chunk in enumerate(chunks):
        start = pl.multiple_of((here + parts - k) % parts * rows, rows)
        out_ref[pl.ds(start, rows), :] = chunk[...]


def assemble(here, chunks):
    rows, width = chunks[0].shape
    return pl.pallas_call(
        lambda here_ref, *refs: put_chunks(here_ref, refs[:-1], refs[-1]),
        out_shape=near((rows * len(chunks), width), bf16),
        in_specs=[SMEM] + [VMEM] * len(chunks),
        out_specs=VMEM,
        cost_estimate=pl.CostEstimate(flops=COST, bytes_accessed=COST, transcendentals=COST),
        compiler_params=pltpu.CompilerParams(vmem_limit_bytes=GRANT),
        name="assemble",
    )(here, *map(keep_near, chunks))


def pick_kernel(first_ref, one_ref, two_ref, out_ref):
    @pl.when(first_ref[0] > 0)
    def _():
        out_ref[...] = one_ref[...]

    @pl.when(first_ref[0] == 0)
    def _():
        out_ref[...] = two_ref[...]


def pick(first, one, two):
    return pl.pallas_call(
        pick_kernel,
        out_shape=near(one.shape, one.dtype),
        in_specs=[SMEM] + [VMEM] * 2,
        out_specs=VMEM,
        cost_estimate=pl.CostEstimate(flops=COST, bytes_accessed=COST, transcendentals=COST),
        compiler_params=pltpu.CompilerParams(vmem_limit_bytes=GRANT),
        name="pick",
    )(first, keep_near(one), keep_near(two))


def frames_kernel(*refs, group, first):
    if first:
        here_ref, chunks = refs[0], refs[1:-4]
        v_ref, ft_ref, w_ref, chain_ref = refs[-4:]
        put_chunks(here_ref, chunks, w_ref)
        base = 0
    else:
        w_ref, old_ref, v_ref, ft_ref, pt_ref, chain_ref = refs
        base = w_ref.shape[0] - v_ref.shape[0]
    heads = w_ref.shape[1] // DH
    steps = v_ref.shape[0] // (SUB * group)
    rows = lax.broadcasted_iota(jnp.int32, (SUB, SUB), 0)
    cols = lax.broadcasted_iota(jnp.int32, (SUB, SUB), 1)
    diagonal = rows == cols
    unit = jnp.where(diagonal, 1.0, 0.0).astype(f32)
    for h in range(heads):
        chain_ref[h] = unit if first else old_ref[h]

    def one(step, carry):
        pairs = [(g, h) for g in range(group) for h in range(heads)]

        def at(g, h):
            start = pl.multiple_of((step * group + g) * SUB, SUB)
            return (pl.ds(start, SUB), pl.ds(h * DH, DH))

        def source(g, h):
            start = pl.multiple_of((step * group + g) * SUB + base, SUB)
            return (pl.ds(start, SUB), pl.ds(h * DH, DH))

        w = [w_ref[source(*p)] for p in pairs]
        wt = [x.T for x in w]
        gram = [dot(x, t) for x, t in zip(w, wt)]
        lower, inverse, matrix = [], [], []
        for x in gram:
            onto = jnp.where(diagonal, x, 0.0)
            down = 2.0 / (jnp.sum(onto, axis=1, keepdims=True) + 1e-6)
            across = 2.0 / (jnp.sum(onto, axis=0, keepdims=True) + 1e-6)
            near = jnp.where((rows == cols + 1) & (rows % 2 == 1), x, 0.0)
            inverse.append(jnp.where(diagonal, down, 0.0) - near * down * across)
            lower.append(halves(x))
            matrix.append(jnp.where(rows > cols, x, jnp.where(diagonal, 0.5 * (x + 1e-6), 0.0)))
        size = 2
        while size < SUB:
            band = (rows // (2 * size) == cols // (2 * size)) & (rows // size > cols // size)
            split = [halves(x) for x in inverse]
            part = [
                (jnp.where(band, x[0], 0).astype(bf16), jnp.where(band, x[1], 0).astype(bf16))
                for x in lower
            ]
            half = [halves(dot3(x, y)) for x, y in zip(split, part)]
            inverse = [x - dot3(y, z) for x, y, z in zip(inverse, half, split)]
            size *= 2
        split = [halves(x) for x in inverse]
        guess = [
            dot(jnp.concatenate(x, axis=1), jnp.concatenate([y, y], axis=0))
            for x, y in zip(split, w)
        ]
        short = [
            (y.astype(f32) - dot6(thirds(m), thirds(x))).astype(bf16)
            for m, x, y in zip(matrix, guess, w)
        ]
        solved = [x + dot(y[0], z) for x, y, z in zip(guess, split, short)]
        whole = [
            thirds(
                unit
                - dot(jnp.concatenate([t, t, t], axis=1), jnp.concatenate(thirds(v), axis=0))
            )
            for t, v in zip(wt, solved)
        ]
        for i, p in enumerate(pairs):
            v_ref[at(*p)] = solved[i]
        frames = [thirds(chain_ref[h]) for h in range(heads)]
        for i, p in enumerate(pairs):
            h = p[1]
            ft_ref[at(*p)] = frames[h][0]
            moved = dot6(whole[i], frames[h])
            if p[0] == group - 1:
                chain_ref[h] = moved
            frames[h] = thirds(moved)
        return carry

    lax.fori_loop(0, steps, one, 0)
    if not first:
        for h in range(heads):
            pt_ref[:, h * DH : (h + 1) * DH] = chain_ref[h].astype(bf16)


def first_frames(here, chunks, group=3):
    rows, width = chunks[0].shape
    rows *= len(chunks)
    half = rows // 2
    return pl.pallas_call(
        lambda *refs: frames_kernel(*refs, group=group, first=True),
        out_shape=(
            near((half, width), f32),
            near((half, width), bf16),
            near((rows, width), bf16),
            near((width // DH, DH, DH), f32),
        ),
        in_specs=[SMEM] + [VMEM] * len(chunks),
        out_specs=(VMEM,) * 4,
        cost_estimate=pl.CostEstimate(flops=COST, bytes_accessed=COST, transcendentals=COST),
        compiler_params=pltpu.CompilerParams(vmem_limit_bytes=GRANT),
        name="first_frames",
    )(here, *map(keep_near, chunks))


def second_frames(w, chain, group=3):
    rows, width = w.shape
    half = rows // 2
    return pl.pallas_call(
        lambda *refs: frames_kernel(*refs, group=group, first=False),
        out_shape=(
            near((half, width), f32),
            near((half, width), bf16),
            near((DH, width), bf16),
        ),
        in_specs=[VMEM] * 2,
        out_specs=(VMEM,) * 3,
        scratch_shapes=[pltpu.VMEM((width // DH, DH, DH), f32)],
        cost_estimate=pl.CostEstimate(flops=COST, bytes_accessed=COST, transcendentals=COST),
        compiler_params=pltpu.CompilerParams(vmem_limit_bytes=GRANT),
        name="second_frames",
    )(keep_near(w), keep_near(chain))


def turn_kernel(here_ref, *refs, group, tail):
    chunks, (w_ref, v0_ref, ft0_ref, v1_ref, ft1_ref, pt_ref, o_ref, x_ref) = refs[:-8], refs[-8:]
    put_chunks(here_ref, chunks, x_ref)
    length, width = x_ref.shape
    heads = width // DH
    half = length // 2
    rows = lax.broadcasted_iota(jnp.int32, (SUB, SUB), 0)
    cols = lax.broadcasted_iota(jnp.int32, (SUB, SUB), 1)
    seen = rows >= cols

    def one(step, base, v_ref, ft_ref):
        places, inner = [], []
        for g in range(group):
            start = pl.multiple_of((step * group + g) * SUB, SUB)
            for h in range(heads):
                inner.append((pl.ds(start, SUB), pl.ds(h * DH, DH)))
                places.append((pl.ds(start + base, SUB), pl.ds(h * DH, DH)))
        x = [x_ref[p] for p in places]
        onto = [thirds(jnp.where(seen, dot_t(y, w_ref[p]), 0.0)) for y, p in zip(x, places)]
        turned = [
            (y.astype(f32) - dot6(z, thirds(v_ref[p]))).astype(bf16)
            for y, z, p in zip(x, onto, inner)
        ]
        for y, p, i in zip(turned, places, inner):
            o_ref[p] = dot(y, ft_ref[i]).astype(bf16)

    for base, v_ref, ft_ref in ((0, v0_ref, ft0_ref), (half, v1_ref, ft1_ref)):

        def loop(step, carry):
            one(step, base, v_ref, ft_ref)
            return carry

        lax.fori_loop(0, half // (SUB * group), loop, 0)
    if tail:
        o_ref[length:, :] = pt_ref[...]


def turn(here, chunks, w, parts, pt, tail, group=2):
    rows, width = w.shape
    return pl.pallas_call(
        lambda *refs: turn_kernel(*refs, group=group, tail=tail),
        out_shape=near((rows + (DH if tail else 0), width), bf16),
        in_specs=[SMEM] + [VMEM] * (6 + len(chunks)),
        out_specs=VMEM,
        scratch_shapes=[pltpu.VMEM((rows, width), bf16)],
        cost_estimate=pl.CostEstimate(flops=COST, bytes_accessed=COST, transcendentals=COST),
        compiler_params=pltpu.CompilerParams(vmem_limit_bytes=GRANT),
        name="turn_keys" if tail else "turn_queries",
    )(here, *map(keep_near, (*chunks, w, *parts, pt)))


SCALE = math.log2(math.e) / math.sqrt(DH)
TILE = 256
SPAN = 256

BLANK = -1e30


def lanes_of(h):
    return slice(h * DH, (h + 1) * DH)


def pack_stats(columns):
    lane = lax.broadcasted_iota(jnp.int32, (columns[0].shape[0], DH), 1)
    out = jnp.zeros(lane.shape, f32)
    for i, c in enumerate(columns):
        out = jnp.where(lane == i, c, out)
    return out


def score(z, k, s_ref, m_ref, start=None):
    s = dot_t(z, k)
    rows, size = s.shape
    if start is not None:
        low = s[:, : size - rows]
        edge = s[:, size - rows :]
        seen = lax.broadcasted_iota(jnp.int32, edge.shape, 0) >= lax.broadcasted_iota(
            jnp.int32, edge.shape, 1
        )
        edge = jnp.where(seen, edge, BLANK)
        s = jnp.concatenate([low, edge], axis=1) if size > rows else edge
    s_ref[:, :size] = s
    m_ref[...] = jnp.broadcast_to(jnp.max(s, axis=1, keepdims=True), m_ref.shape)


def weigh(v, s_ref, m_ref):
    size = v.shape[0]
    best = m_ref[:, :1]
    p = jnp.exp2((s_ref[:, :size] - best) * SCALE).astype(bf16)
    return best, dot(p, jnp.concatenate([v, jnp.ones_like(v)], axis=1))


def scratch(heads, length, tile):
    return [pltpu.VMEM((tile, length), f32) for _ in range(heads)] + [
        pltpu.VMEM((tile, DH), f32) for _ in range(heads)
    ]


def local_kernel(q_ref, k_ref, v_ref, acc_ref, stat_ref, *work):
    length, width = q_ref.shape
    heads = width // DH
    tiles = length // TILE

    def first(i, h):
        size = (i + 1) * TILE
        score(
            q_ref[i * TILE : size, lanes_of(h)],
            k_ref[:size, lanes_of(h)],
            work[h],
            work[heads + h],
            i * TILE,
        )

    order = [(i, h) for i in range(tiles) for h in range(heads)]
    first(*order[0])
    columns = []
    for n, (i, h) in enumerate(order):
        if n + 1 < len(order):
            first(*order[n + 1])
        size = (i + 1) * TILE
        best, both = weigh(v_ref[:size, lanes_of(h)], work[h], work[heads + h])
        acc_ref[i * TILE : size, lanes_of(h)] = both[:, :DH]
        columns += [best, both[:, DH : DH + 1]]
        if h == heads - 1:
            stat_ref[i * TILE : size, :] = pack_stats(columns)
            columns = []


def attend_local(zq, kp, v):
    rows, width = zq.shape
    return pl.pallas_call(
        local_kernel,
        out_shape=(
            near((rows, width), f32),
            near((rows, DH), f32),
        ),
        in_specs=[VMEM] * 3,
        out_specs=(VMEM,) * 2,
        scratch_shapes=scratch(width // DH, rows, TILE),
        cost_estimate=pl.CostEstimate(flops=COST, bytes_accessed=COST, transcendentals=COST),
        compiler_params=pltpu.CompilerParams(vmem_limit_bytes=GRANT),
        name="attend_local",
    )(keep_near(zq), keep_near(kp), keep_near(v))


def merge(ok, best, both, stat, acc, h, wide):
    old = stat[:, 2 * h : 2 * h + 1]
    top = jnp.where(ok, jnp.maximum(old, best), old)
    keep = jnp.exp2((old - top) * SCALE)
    gain = jnp.where(ok, jnp.exp2((best - top) * SCALE), 0.0)
    sums = both[:, DH:] if wide else both[:, DH : DH + 1]
    total = stat[:, 2 * h + 1 : 2 * h + 2] * keep + sums * gain
    return top, acc * keep + both[:, :DH] * gain, total


def hop_kernel(ok_ref, z_ref, k_ref, v_ref, acc_ref, stat_ref, out_ref, total_ref, turned_ref, *work):
    length, width = z_ref.shape
    heads = width // DH
    tiles = length // SPAN
    ok = ok_ref[0] > 0
    for h in range(heads):
        turned_ref[:, lanes_of(h)] = dot(z_ref[:, lanes_of(h)], k_ref[length:, lanes_of(h)]).astype(
            bf16
        )

    def rows_of(i):
        return pl.ds(pl.multiple_of(i * SPAN, SPAN), SPAN)

    def first(i, h):
        score(turned_ref[rows_of(i), lanes_of(h)], k_ref[:length, lanes_of(h)], work[h], work[heads + h])

    def one(i, more):
        columns = []
        for h in range(heads):
            if h + 1 < heads:
                first(i, h + 1)
            elif more:
                first(i + 1, 0)
            best, both = weigh(v_ref[:, lanes_of(h)], work[h], work[heads + h])
            top, acc, total = merge(
                ok, best, both, stat_ref[rows_of(i), :], acc_ref[rows_of(i), lanes_of(h)], h, False
            )
            out_ref[rows_of(i), lanes_of(h)] = acc
            columns += [top, total]
        total_ref[rows_of(i), :] = pack_stats(columns)

    first(0, 0)

    def step(i, carry):
        one(i, True)
        return carry

    lax.fori_loop(0, tiles - 1, step, 0)
    one(tiles - 1, False)


def attend_hop(ok, z, kp, v, acc, stat):
    rows, width = z.shape
    return pl.pallas_call(
        hop_kernel,
        out_shape=(near((rows, width), f32), near((rows, DH), f32), near((rows, width), bf16)),
        in_specs=[SMEM] + [VMEM] * 5,
        out_specs=(VMEM,) * 3,
        scratch_shapes=scratch(width // DH, rows, SPAN),
        cost_estimate=pl.CostEstimate(flops=COST, bytes_accessed=COST, transcendentals=COST),
        compiler_params=pltpu.CompilerParams(vmem_limit_bytes=GRANT),
        name="attend_hop",
    )(ok, *map(keep_near, (z, kp, v, acc, stat)))


def last_kernel(ok_ref, here_ref, z_ref, *refs, targets, parts):
    pairs, refs = (refs[:2], refs[2:4]), refs[4:]
    acc_ref, stat_ref, out, work = refs[0], refs[1], refs[2 : 2 + len(targets)], refs[2 + len(targets) :]
    done_ref, turned_ref, work = work[0], work[1], work[2:]
    length, width = z_ref.shape
    heads = width // DH
    piece = length // parts
    order = [(d, h) for d in range(len(pairs)) for h in range(heads)]

    def rows_of(i):
        return pl.ds(pl.multiple_of((here_ref[0] + targets[0] + i) % parts * piece, piece), piece)

    def first(i, d, h):
        k_ref = pairs[d][0]
        old = turned_ref[:, lanes_of(h)] if d else z_ref[rows_of(i), lanes_of(h)]
        z = dot(old, k_ref[length:, lanes_of(h)]).astype(bf16)
        turned_ref[:, lanes_of(h)] = z
        score(z, k_ref[:length, lanes_of(h)], work[h], work[heads + h])

    def one(i, carry):
        state = [None] * heads
        for n, (d, h) in enumerate(order):
            if n + 1 < len(order):
                first(i, *order[n + 1])
            elif len(targets) > 1:
                first(jnp.minimum(i + 1, len(targets) - 1), *order[0])
            best, both = weigh(pairs[d][1][:, lanes_of(h)], work[h], work[heads + h])
            if d == 0:
                stat = stat_ref[rows_of(i), :]
                old = stat[:, 2 * h : 2 * h + 1]
                total = stat[:, 2 * h + 1 : 2 * h + 2]
                acc = acc_ref[rows_of(i), lanes_of(h)]
            else:
                old, acc, total = state[h]
            ok = ok_ref[d] > 0
            top = jnp.where(ok, jnp.maximum(old, best), old)
            keep = jnp.exp2((old - top) * SCALE)
            gain = jnp.where(ok, jnp.exp2((best - top) * SCALE), 0.0)
            acc = acc * keep + both[:, :DH] * gain
            total = total * keep + both[:, DH:] * gain
            state[h] = (top, acc, total)
            if d == len(pairs) - 1:
                done_ref[i, :, lanes_of(h)] = (acc / total).astype(bf16)
        return carry

    first(0, *order[0])
    lax.fori_loop(0, len(targets), one, 0)
    for i in range(len(targets)):
        out[i][...] = done_ref[i]


def attend_last(ok, here, z, near_pair, far_pair, acc, stat, targets, parts):
    rows, width = z.shape
    piece = rows // parts
    return pl.pallas_call(
        lambda *refs: last_kernel(*refs, targets=targets, parts=parts),
        out_shape=tuple(near((piece, width), bf16) for _ in targets),
        in_specs=[SMEM] * 2 + [VMEM] * 7,
        out_specs=(VMEM,) * len(targets),
        scratch_shapes=[
            pltpu.VMEM((len(targets), piece, width), bf16),
            pltpu.VMEM((piece, width), bf16),
        ]
        + scratch(width // DH, rows, piece),
        cost_estimate=pl.CostEstimate(flops=COST, bytes_accessed=COST, transcendentals=COST),
        compiler_params=pltpu.CompilerParams(vmem_limit_bytes=GRANT),
    )(ok, here, *map(keep_near, (z, *near_pair, *far_pair, acc, stat)))


HOPS = 3
CORES = 2
LINE = 4


def shift(value, axis, by):
    length = lax.axis_size(axis)
    return lax.ppermute(value, axis, [(i, (i + by) % length) for i in range(length)])


def exchange(array, axis):
    parts = lax.axis_size("head")
    here = lax.axis_index("head")
    size = array.shape[axis] // parts
    pieces = [
        lax.dynamic_slice_in_dim(array, (here + k) % parts * size, size, axis)
        for k in range(parts)
    ]
    return pieces[:1] + [shift(piece, "head", k) for k, piece in enumerate(pieces) if k]


def relays(length):
    back, onto, inside = [], [], []
    for c in range(CORES - 1, length, CORES):
        row, chip = divmod(c // CORES, LINE)
        relay = (row * LINE + (chip - 1) % LINE) * CORES + CORES - 1
        back.append((c, relay))
        onto.append((relay, (c + HOPS) % length))
        inside.append((c - 1, c))
    return back, onto, inside


def ring(value):
    back, onto, inside = relays(lax.axis_size("ctx"))
    one = shift(value, "ctx", 1)
    passed = lax.ppermute(value, "ctx", back)
    two = shift(one, "ctx", 1)
    far = lax.ppermute(passed, "ctx", onto)
    close = lax.ppermute(two, "ctx", inside)
    far_side = (lax.axis_index("ctx") % CORES == 0).astype(jnp.int32).reshape(1)
    return one, two, pick(far_side, far, close)


def body(queries, keys, values, directions):
    parts = lax.axis_size("head")
    here = lax.axis_index("head").astype(jnp.int32).reshape(1)
    position = lax.axis_index("ctx")
    oks = [(position >= d).astype(jnp.int32).reshape(1) for d in range(1, HOPS + 1)]
    w = exchange(directions, 1)
    v = exchange(values, 1)
    k = exchange(keys, 1)
    q = exchange(queries, 1)
    v = assemble(here, v)
    low_a, ft_a, w, chain = first_frames(here, w)
    low_b, ft_b, pt = second_frames(w, chain)
    frames = (low_a, ft_a, low_b, ft_b)
    kp = turn(here, k, w, frames, pt, True)
    z = turn(here, q, w, frames, pt, False)
    acc, stat = attend_local(z, kp, v)
    vs = ring(v)
    ks = ring(kp)
    acc, stat, z = attend_hop(oks[0], z, ks[0], vs[0], acc, stat)
    state = (jnp.concatenate(oks[1:]), here, z, (ks[1], vs[1]), (ks[2], vs[2]), acc, stat)
    pieces = attend_last(*state, tuple(range(1, parts)), parts)
    pieces = [shift(piece, "head", k + 1) for k, piece in enumerate(pieces)]
    pieces = list(attend_last(*state, (0,), parts)) + pieces
    rows, width = pieces[0].shape
    result = jnp.zeros((rows, width * parts), bf16)
    for k, piece in enumerate(pieces):
        result = lax.dynamic_update_slice(result, piece, (0, (here[0] + parts - k) % parts * width))
    return result


def solution(mesh):
    spec = P(("ctx", "head"), None)
    return jax.shard_map(
        body, mesh=mesh, in_specs=(spec,) * 4, out_specs=spec, check_vma=False
    )
```

time: 180 us -> 167 us (0.928)
  Pallas kernels: 75.5 us -> 60.5 us
  starting transfers between devices: 24.1 us -> 34.2 us
  waiting for transfers between devices: 62 us -> 54.2 us
    pallas_call x5 -> x9, Pallas kernels: 65.6 us -> 52 us  [the longest x2 18.2 us: attend_last(): pl.pallas_call(lambda *refs: last_kernel(*refs, targets=targets, parts=pa...]
    ppermute x0 -> x6, starting transfers between devices: none -> 10.2 us  [the longest x2 4.46 us: ring(): close = lax.ppermute(two, 'ctx', inside)]
    unnamed x20 -> x48, local copies, waits for them, and re-layouts: 3.51 us -> 13.2 us
    ppermute x21 -> x19, waiting for transfers between devices: 62 us -> 54.2 us  [shift(): lax.ppermute(value, axis, [(i, (i + by) % length) for i in range(length)])]
    dynamic_update_slice x15 -> x4, local copies, waits for them, and re-layouts: 7.5 us -> 0.75 us  [body(): lax.dynamic_update_slice(result, piece, (0, (here[0] + parts - k) % parts...]
    dynamic_slice x5 -> x4, local copies, waits for them, and re-layouts: 6.01 us -> 3.13 us  [exchange(): lax.dynamic_slice_in_dim(array, (here + k) % parts * size, size, axis)]
    ppermute x21 -> x19, starting transfers between devices: 24.1 us -> 24.1 us  [shift(): lax.ppermute(value, axis, [(i, (i + by) % length) for i in range(length)])]
  transfers between devices with their start and end apart: 21 -> 25, of which waited for: 8 -> 9; matrix products, arithmetic and copies ran while one was open for 5% -> 1% of each run, Pallas kernels for 35% -> 27%
where the time goes in v2:
time: 167 us
  Pallas kernels  60.5 us (36%)
  waiting for transfers between devices  54.2 us (32%)
  starting transfers between devices  34.2 us (20%)
  local copies, waits for them, and re-layouts  17.2 us (10%)
    ppermute x19, waiting for transfers between devices, shift(): lax.ppermute(value, axis, [(i, (i + by) % length) for i in range(length)])  54.2 us
    ppermute x19, starting transfers between devices, shift(): lax.ppermute(value, axis, [(i, (i + by) % length) for i in range(length)])  24.1 us
    pallas_call x2, Pallas kernels, attend_last(): pl.pallas_call(lambda *refs: last_kernel(*refs, targets=targets, parts=pa...  18.2 us
    unnamed x48, local copies, waits for them, and re-layouts  13.2 us
    pallas_call x1, Pallas kernels, attend_hop(): pl.pallas_call(hop_kernel, out_shape=(near((rows, width), f32), near((row...  9.23 us
    pallas_call x2, Pallas kernels, turn(): pl.pallas_call(lambda *refs: turn_kernel(*refs, group=group, tail=tail),...  8.51 us
    pallas_call x1, Pallas kernels, first_frames(): pl.pallas_call(lambda *refs: frames_kernel(*refs, group=group, first=True...  7.46 us
    pallas_call x1, Pallas kernels, second_frames(): pl.pallas_call(lambda *refs: frames_kernel(*refs, group=group, first=Fals...  7.43 us
  transfers between devices with their start and end apart: 25, of which 9 were waited for; matrix products, arithmetic and copies ran while one was open for 1% of the time, Pallas kernels for 27%

profile of v2, /device:TPU:0, one launch (start us, length us, event | category | flops | bytes accessed | tf_op | source)
XLA Modules:
  0.0 166.6 jit_solution(8104399990199240661)
XLA Ops:
  0.0 1.4 constant_dynamic-slice_fusion.8
  1.4 2.1 %collective-permute-start.3 = (bf16[384,256]{1,0:T(8,128)(2,1)S(1)}, bf16[384,256]{1,0:T(8,128)(2,1)S(1)}, u32[]{:S(2)}, u32[]{:S(2)}) collective-permute-start(bf16[384,256]{1,0:T(8,128)(2,1)S(1)} %get-tuple-element.44), channel_id=1, source_target_pairs={{0,1},{1,2},{2,3},{3,0},{4,5},{5,6},{6,7},{7,4},{8,9},{9,10},{10,1... | collective-permute-start | bytes 589832 | tf_op jit(solution)/shard_map/ppermute | solution.py:515
  3.5 3.6 %collective-permute-start.4 = (bf16[384,256]{1,0:T(8,128)(2,1)S(1)}, bf16[384,256]{1,0:T(8,128)(2,1)S(1)}, u32[]{:S(2)}, u32[]{:S(2)}) collective-permute-start(bf16[384,256]{1,0:T(8,128)(2,1)S(1)} %get-tuple-element.46), channel_id=1, source_target_pairs={{0,2},{1,3},{2,0},{3,1},{4,6},{5,7},{6,4},{7,5},{8,10},{9,11},{10,... | collective-permute-start | bytes 589832 | tf_op jit(solution)/shard_map/ppermute | solution.py:515
  10.5 2.9 %collective-permute-start.8 = (bf16[384,256]{1,0:T(8,128)(2,1)S(1)}, bf16[384,256]{1,0:T(8,128)(2,1)S(1)}, u32[]{:S(2)}, u32[]{:S(2)}) collective-permute-start(bf16[384,256]{1,0:T(8,128)(2,1)S(1)} %get-tuple-element.39), channel_id=1, source_target_pairs={{0,3},{1,0},{2,1},{3,2},{4,7},{5,4},{6,5},{7,6},{8,11},{9,8},{10,9... | collective-permute-start | bytes 589832 | tf_op jit(solution)/shard_map/ppermute | solution.py:515
  14.2 2.8 %collective-permute-done.4.refs_3_ = bf16[384,256]{1,0:T(8,128)(2,1)S(1)} collective-permute-done((bf16[384,256]{1,0:T(8,128)(2,1)S(1)}, bf16[384,256]{1,0:T(8,128)(2,1)S(1)}, u32[]{:S(2)}, u32[]{:S(2)}) %collective-permute-start.4) | collective-permute-done | bytes 196640 | tf_op jit(solution)/shard_map/ppermute | solution.py:515
  17.1 3.2 %collective-permute-start.11 = (bf16[384,256]{1,0:T(8,128)(2,1)}, bf16[384,256]{1,0:T(8,128)(2,1)}, u32[]{:S(2)}, u32[]{:S(2)}) collective-permute-start(bf16[384,256]{1,0:T(8,128)(2,1)} %get-tuple-element.38), channel_id=1, source_target_pairs={{0,2},{1,3},{2,0},{3,1},{4,6},{5,7},{6,4},{7,5},{8,10},{9,11},{10,... | collective-permute-start | bytes 589832 | tf_op jit(solution)/shard_map/ppermute | solution.py:515
  20.3 7.5 %first_frames.1 = (f32[768,256]{1,0:T(8,128)S(1)}, bf16[768,256]{1,0:T(8,128)(2,1)S(1)}, bf16[1536,256]{1,0:T(8,128)(2,1)S(1)}, f32[2,128,128]{2,1,0:T(8,128)S(1)}) custom-call(s32[1]{0:T(128)} %bitcast.2.refs_0_.here_ref.refs_1_, bf16[384,256]{1,0:T(8,128)(2,1)S(1)} %get-tuple-element.45.refs_1_, bf16[384,256]{1,0:T(8,128)(2,1)S(1)} %collective-permute-done.3.refs_2_, ...), custom_call_target="tpu_custom_call" | custom-call | flops 100000000 | bytes 100000000 | tf_op jit(solution)/shard_map/first_frames/pallas_call | solution.py:194
  27.8 1.4 collective-permute-start.12
  29.2 7.4 %second_frames.1 = (f32[768,256]{1,0:T(8,128)S(1)}, bf16[768,256]{1,0:T(8,128)(2,1)S(1)}, bf16[128,256]{1,0:T(8,128)(2,1)S(1)}) custom-call(bf16[1536,256]{1,0:T(8,128)(2,1)S(1)} %get-tuple-element.20.refs_0_.refs_5_, f32[2,128,128]{2,1,0:T(8,128)S(1)} %get-tuple-element.23.refs_1_), custom_call_target="tpu_custom_call" | custom-call | flops 100000000 | bytes 100000000 | tf_op jit(solution)/shard_map/second_frames/pallas_call | solution.py:213
  36.7 3.8 %turn_keys.1.k_ref = bf16[1664,256]{1,0:T(8,128)(2,1)S(1)} custom-call(s32[1]{0:T(128)} %bitcast.2.refs_0_.here_ref.refs_1_, bf16[384,256]{1,0:T(8,128)(2,1)S(1)} %get-tuple-element.41.refs_1_, bf16[384,256]{1,0:T(8,128)(2,1)S(1)} %collective-permute-done.6.refs_2_, bf16[384,256]{1,0:T(8,128)(2,1)S(1)} %collective-permute-done.7.refs_3_, ...), custom_call_target="tpu_custom_call" | custom-call | flops 100000000 | bytes 100000000 | tf_op jit(solution)/shard_map/turn_keys/pallas_call | solution.py:268
  42.0 1.7 %collective-permute-start.13 = (bf16[1536,256]{1,0:T(8,128)(2,1)S(1)}, bf16[1536,256]{1,0:T(8,128)(2,1)S(1)}, u32[]{:S(2)}, u32[]{:S(2)}) collective-permute-start(bf16[1536,256]{1,0:T(8,128)(2,1)S(1)} %assemble.1.v_ref), channel_id=1, source_target_pairs={{0,4},{4,8},{8,12},{12,16},{16,20},{20,24},{24,28},{28,32},{32,36}... | collective-permute-start | bytes 2359304 | tf_op jit(solution)/shard_map/ppermute | solution.py:515
  43.8 1.6 collective-permute-start.16
  45.3 10.9 %collective-permute-done.9.k_ref = bf16[1664,256]{1,0:T(8,128)(2,1)S(1)} collective-permute-done((bf16[1664,256]{1,0:T(8,128)(2,1)S(1)}, bf16[1664,256]{1,0:T(8,128)(2,1)S(1)}, u32[]{:S(2)}, u32[]{:S(2)}) %collective-permute-start.9) | collective-permute-done | bytes 852000 | tf_op jit(solution)/shard_map/ppermute | solution.py:515
  56.3 1.6 collective-permute-start.19
  57.8 6.9 %collective-permute-done.13.v_ref = bf16[1536,256]{1,0:T(8,128)(2,1)S(1)} collective-permute-done((bf16[1536,256]{1,0:T(8,128)(2,1)S(1)}, bf16[1536,256]{1,0:T(8,128)(2,1)S(1)}, u32[]{:S(2)}, u32[]{:S(2)}) %collective-permute-start.13) | collective-permute-done | bytes 786464 | tf_op jit(solution)/shard_map/ppermute | solution.py:515
  66.0 7.9 %collective-permute-done.14.refs_3_ = bf16[1664,256]{1,0:T(8,128)(2,1)} collective-permute-done((bf16[1664,256]{1,0:T(8,128)(2,1)S(1)}, bf16[1664,256]{1,0:T(8,128)(2,1)}, u32[]{:S(2)}, u32[]{:S(2)}) %collective-permute-start.14) | collective-permute-done | bytes 852000 | tf_op jit(solution)/shard_map/ppermute | solution.py:515
  73.9 2.2 %collective-permute-start.18 = (bf16[1664,256]{1,0:T(8,128)(2,1)}, bf16[1664,256]{1,0:T(8,128)(2,1)}, u32[]{:S(2)}, u32[]{:S(2)}) collective-permute-start(bf16[1664,256]{1,0:T(8,128)(2,1)} %collective-permute-done.14.refs_3_), channel_id=1, source_target_pairs={{0,4},{8,12},{16,20},{24,28},{32,36},{40,44},{48,52},{56,60},{64,6... | collective-permute-start | bytes 2555912 | tf_op jit(solution)/shard_map/ppermute | solution.py:546
  77.4 4.9 %collective-permute-done.15.refs_4_ = bf16[1536,256]{1,0:T(8,128)(2,1)} collective-permute-done((bf16[1536,256]{1,0:T(8,128)(2,1)S(1)}, bf16[1536,256]{1,0:T(8,128)(2,1)}, u32[]{:S(2)}, u32[]{:S(2)}) %collective-permute-start.15) | collective-permute-done | bytes 786464 | tf_op jit(solution)/shard_map/ppermute | solution.py:515
  82.3 2.2 %collective-permute-start.21 = (bf16[1536,256]{1,0:T(8,128)(2,1)}, bf16[1536,256]{1,0:T(8,128)(2,1)}, u32[]{:S(2)}, u32[]{:S(2)}) collective-permute-start(bf16[1536,256]{1,0:T(8,128)(2,1)} %collective-permute-done.15.refs_4_), channel_id=1, source_target_pairs={{0,4},{8,12},{16,20},{24,28},{32,36},{40,44},{48,52},{56,60},{64,6... | collective-permute-start | bytes 2359304 | tf_op jit(solution)/shard_map/ppermute | solution.py:546
  86.1 8.3 %collective-permute-done.refs_2_ = bf16[384,256]{1,0:T(8,128)(2,1)S(1)} collective-permute-done((bf16[384,256]{1,0:T(8,128)(2,1)S(1)}, bf16[384,256]{1,0:T(8,128)(2,1)S(1)}, u32[]{:S(2)}, u32[]{:S(2)}) %collective-permute-start) | collective-permute-done | bytes 196640 | tf_op jit(solution)/shard_map/ppermute | solution.py:515
  95.1 7.2 %collective-permute-done.1.refs_3_ = bf16[384,256]{1,0:T(8,128)(2,1)S(1)} collective-permute-done((bf16[384,256]{1,0:T(8,128)(2,1)S(1)}, bf16[384,256]{1,0:T(8,128)(2,1)S(1)}, u32[]{:S(2)}, u32[]{:S(2)}) %collective-permute-start.1) | collective-permute-done | bytes 196640 | tf_op jit(solution)/shard_map/ppermute | solution.py:515
  102.9 1.5 collective-permute-start.2
  104.4 4.5 %collective-permute-done.2.refs_4_ = bf16[384,256]{1,0:T(8,128)(2,1)} collective-permute-done((bf16[384,256]{1,0:T(8,128)(2,1)}, bf16[384,256]{1,0:T(8,128)(2,1)}, u32[]{:S(2)}, u32[]{:S(2)}) %collective-permute-start.2) | collective-permute-done | bytes 196640 | tf_op jit(solution)/shard_map/ppermute | solution.py:515
  116.1 4.7 %turn_queries.1.q_ref.z_ref = bf16[1536,256]{1,0:T(8,128)(2,1)S(1)} custom-call(s32[1]{0:T(128)} %bitcast.2.refs_0_.here_ref.refs_1_, bf16[384,256]{1,0:T(8,128)(2,1)S(1)} %get-tuple-element.49.refs_1_, bf16[384,256]{1,0:T(8,128)(2,1)S(1)} %copy-done.1, bf16[384,256]{1,0:T(8,128)(2,1)S(1)} %copy-done.3, bf16[384,256]{1,0:T(8,128)(2,1)} %collective-permute-done.2.refs_4_, ...), custom_call_target="tpu_custom_call" | custom-call | flops 100000000 | bytes 100000000 | tf_op jit(solution)/shard_map/turn_queries/pallas_call | solution.py:268
  120.9 4.3 %attend_local.1 = (f32[1536,256]{1,0:T(8,128)S(1)}, f32[1536,128]{1,0:T(8,128)S(1)}) custom-call(bf16[1536,256]{1,0:T(8,128)(2,1)S(1)} %turn_queries.1.q_ref.z_ref, bf16[1664,256]{1,0:T(8,128)(2,1)S(1)} %turn_keys.1.k_ref, bf16[1536,256]{1,0:T(8,128)(2,1)S(1)} %assemble.1.v_ref), custom_call_target="tpu_custom_call" | custom-call | flops 100000000 | bytes 100000000 | tf_op jit(solution)/shard_map/attend_local/pallas_call | solution.py:359
  125.1 9.2 %attend_hop.1 = (f32[1536,256]{1,0:T(8,128)S(1)}, f32[1536,128]{1,0:T(8,128)S(1)}, bf16[1536,256]{1,0:T(8,128)(2,1)S(1)}) custom-call(s32[1]{0:T(128)} %bitcast.3.ok_ref, bf16[1536,256]{1,0:T(8,128)(2,1)S(1)} %turn_queries.1.q_ref.z_ref, bf16[1664,256]{1,0:T(8,128)(2,1)S(1)} %collective-permute-done.9.k_ref, ...), custom_call_target="tpu_custom_call" | custom-call | flops 100000000 | bytes 100000000 | tf_op jit(solution)/shard_map/attend_hop/pallas_call | solution.py:427
  134.4 2.3 %pick.3.refs_6_ = bf16[1536,256]{1,0:T(8,128)(2,1)S(1)} custom-call(s32[1]{0:T(128)} %bitcast.4.first_ref, bf16[1536,256]{1,0:T(8,128)(2,1)} %collective-permute-done.20.one_ref, bf16[1536,256]{1,0:T(8,128)(2,1)} %collective-permute-done.21.two_ref), custom_call_target="tpu_custom_call" | custom-call | flops 100000000 | bytes 100000000 | tf_op jit(solution)/shard_map/pick/pallas_call | solution.py:92
  136.7 2.0 %pick.2.refs_5_ = bf16[1664,256]{1,0:T(8,128)(2,1)S(1)} custom-call(s32[1]{0:T(128)} %bitcast.4.first_ref, bf16[1664,256]{1,0:T(8,128)(2,1)} %collective-permute-done.17.one_ref, bf16[1664,256]{1,0:T(8,128)(2,1)} %collective-permute-done.18.two_ref), custom_call_target="tpu_custom_call" | custom-call | flops 100000000 | bytes 100000000 | tf_op jit(solution)/shard_map/pick/pallas_call | solution.py:92
  138.7 13.0 %shard_map.47 = (bf16[384,256]{1,0:T(8,128)(2,1)S(1)}, bf16[384,256]{1,0:T(8,128)(2,1)S(1)}, bf16[384,256]{1,0:T(8,128)(2,1)S(1)}) custom-call(s32[2]{0:T(128)S(1)} %add_convert_fusion.refs_0_, s32[1]{0:T(128)} %bitcast.2.refs_0_.here_ref.refs_1_, bf16[1536,256]{1,0:T(8,128)(2,1)S(1)} %get-tuple-element.29.refs_2_, ...), custom_call_target="tpu_custom_call" | custom-call | flops 100000000 | bytes 100000000 | tf_op jit(solution)/shard_map/pallas_call | solution.py:493
  151.8 4.1 %collective-permute-start.23 = (bf16[384,256]{1,0:T(8,128)(2,1)S(1)}, bf16[384,256]{1,0:T(8,128)(2,1)S(1)}, u32[]{:S(2)}, u32[]{:S(2)}) collective-permute-start(bf16[384,256]{1,0:T(8,128)(2,1)S(1)} %get-tuple-element.33), channel_id=1, source_target_pairs={{0,2},{1,3},{2,0},{3,1},{4,6},{5,7},{6,4},{7,5},{8,10},{9,11},{10,... | collective-permute-start | bytes 589832 | tf_op jit(solution)/shard_map/ppermute | solution.py:515
  155.9 1.4 copy-done.5
  159.5 5.3 %shard_map.46 = bf16[384,256]{1,0:T(8,128)(2,1)S(1)} custom-call(s32[2]{0:T(128)S(1)} %add_convert_fusion.refs_0_, s32[1]{0:T(128)} %bitcast.2.refs_0_.here_ref.refs_1_, bf16[1536,256]{1,0:T(8,128)(2,1)S(1)} %copy-done.7, bf16[1664,256]{1,0:T(8,128)(2,1)} %collective-permute-done.14.refs_3_, bf16[1536,256]{1,0:T(8,128)(2,1)} %collective-permute-done.15.refs_4_, ...), custom_call_target="tpu_custom_call" | custom-call | flops 100000000 | bytes 100000000 | tf_op jit(solution)/shard_map/pallas_call | solution.py:493
  (87 shorter events, 22.6 us)
Async XLA Ops:
  0.0 8.1 %copy-start.20 = (bf16[384,1024]{1,0:T(8,128)(2,1)S(1)}, bf16[384,1024]{1,0:T(8,128)(2,1)}, u32[]{:S(2)}) copy-start(bf16[384,1024]{1,0:T(8,128)(2,1)} %param.5) | copy-start | bytes 2359300
  0.0 13.4 %copy-start.21 = (bf16[384,1024]{1,0:T(8,128)(2,1)S(1)}, bf16[384,1024]{1,0:T(8,128)(2,1)}, u32[]{:S(2)}) copy-start(bf16[384,1024]{1,0:T(8,128)(2,1)} %param.6) | copy-start | bytes 2359300
  1.4 9.1 %collective-permute-start.3 = (bf16[384,256]{1,0:T(8,128)(2,1)S(1)}, bf16[384,256]{1,0:T(8,128)(2,1)S(1)}, u32[]{:S(2)}, u32[]{:S(2)}) collective-permute-start(bf16[384,256]{1,0:T(8,128)(2,1)S(1)} %get-tuple-element.44), channel_id=1, source_target_pairs={{0,1},{1,2},{2,3},{3,0},{4,5},{5,6},{6,7},{7,4},{8,9},{9,10},{10,1... | collective-permute-start | bytes 589832 | tf_op jit(solution)/shard_map/ppermute | solution.py:515
  3.5 13.6 %collective-permute-start.4 = (bf16[384,256]{1,0:T(8,128)(2,1)S(1)}, bf16[384,256]{1,0:T(8,128)(2,1)S(1)}, u32[]{:S(2)}, u32[]{:S(2)}) collective-permute-start(bf16[384,256]{1,0:T(8,128)(2,1)S(1)} %get-tuple-element.46), channel_id=1, source_target_pairs={{0,2},{1,3},{2,0},{3,1},{4,6},{5,7},{6,4},{7,5},{8,10},{9,11},{10,... | collective-permute-start | bytes 589832 | tf_op jit(solution)/shard_map/ppermute | solution.py:515
  7.1 10.0 %collective-permute-start.5 = (bf16[384,256]{1,0:T(8,128)(2,1)S(1)}, bf16[384,256]{1,0:T(8,128)(2,1)S(1)}, u32[]{:S(2)}, u32[]{:S(2)}) collective-permute-start(bf16[384,256]{1,0:T(8,128)(2,1)S(1)} %get-tuple-element.43), channel_id=1, source_target_pairs={{0,3},{1,0},{2,1},{3,2},{4,7},{5,4},{6,5},{7,6},{8,11},{9,8},{10,9... | collective-permute-start | bytes 589832 | tf_op jit(solution)/shard_map/ppermute | solution.py:515
  8.2 19.6 %collective-permute-start.6 = (bf16[384,256]{1,0:T(8,128)(2,1)S(1)}, bf16[384,256]{1,0:T(8,128)(2,1)S(1)}, u32[]{:S(2)}, u32[]{:S(2)}) collective-permute-start(bf16[384,256]{1,0:T(8,128)(2,1)S(1)} %get-tuple-element.40), channel_id=1, source_target_pairs={{0,1},{1,2},{2,3},{3,0},{4,5},{5,6},{6,7},{7,4},{8,9},{9,10},{10,1... | collective-permute-start | bytes 589832 | tf_op jit(solution)/shard_map/ppermute | solution.py:515
  9.3 27.4 %collective-permute-start.7 = (bf16[384,256]{1,0:T(8,128)(2,1)S(1)}, bf16[384,256]{1,0:T(8,128)(2,1)S(1)}, u32[]{:S(2)}, u32[]{:S(2)}) collective-permute-start(bf16[384,256]{1,0:T(8,128)(2,1)S(1)} %get-tuple-element.42), channel_id=1, source_target_pairs={{0,2},{1,3},{2,0},{3,1},{4,6},{5,7},{6,4},{7,5},{8,10},{9,11},{10,... | collective-permute-start | bytes 589832 | tf_op jit(solution)/shard_map/ppermute | solution.py:515
  10.5 26.2 %collective-permute-start.8 = (bf16[384,256]{1,0:T(8,128)(2,1)S(1)}, bf16[384,256]{1,0:T(8,128)(2,1)S(1)}, u32[]{:S(2)}, u32[]{:S(2)}) collective-permute-start(bf16[384,256]{1,0:T(8,128)(2,1)S(1)} %get-tuple-element.39), channel_id=1, source_target_pairs={{0,3},{1,0},{2,1},{3,2},{4,7},{5,4},{6,5},{7,6},{8,11},{9,8},{10,9... | collective-permute-start | bytes 589832 | tf_op jit(solution)/shard_map/ppermute | solution.py:515
  17.1 23.7 %collective-permute-start.10 = (bf16[384,256]{1,0:T(8,128)(2,1)}, bf16[384,256]{1,0:T(8,128)(2,1)}, u32[]{:S(2)}, u32[]{:S(2)}) collective-permute-start(bf16[384,256]{1,0:T(8,128)(2,1)} %get-tuple-element.36), channel_id=1, source_target_pairs={{0,1},{1,2},{2,3},{3,0},{4,5},{5,6},{6,7},{7,4},{8,9},{9,10},{10,1... | collective-permute-start | bytes 589832 | tf_op jit(solution)/shard_map/ppermute | solution.py:515
  17.1 23.8 %collective-permute-start.11 = (bf16[384,256]{1,0:T(8,128)(2,1)}, bf16[384,256]{1,0:T(8,128)(2,1)}, u32[]{:S(2)}, u32[]{:S(2)}) collective-permute-start(bf16[384,256]{1,0:T(8,128)(2,1)} %get-tuple-element.38), channel_id=1, source_target_pairs={{0,2},{1,3},{2,0},{3,1},{4,6},{5,7},{6,4},{7,5},{8,10},{9,11},{10,... | collective-permute-start | bytes 589832 | tf_op jit(solution)/shard_map/ppermute | solution.py:515
  27.8 8.9 %copy-start.10 = (f32[768,256]{1,0:T(8,128)}, f32[768,256]{1,0:T(8,128)S(1)}, u32[]{:S(2)}) copy-start(f32[768,256]{1,0:T(8,128)S(1)} %get-tuple-element.21.refs_6_) | copy-start | bytes 2359300
  27.8 8.9 %copy-start.12 = (bf16[1536,256]{1,0:T(8,128)(2,1)}, bf16[1536,256]{1,0:T(8,128)(2,1)S(1)}, u32[]{:S(2)}) copy-start(bf16[1536,256]{1,0:T(8,128)(2,1)S(1)} %get-tuple-element.20.refs_0_.refs_5_) | copy-start | bytes 2359300
  27.8 8.9 %copy-start.16 = (bf16[768,256]{1,0:T(8,128)(2,1)}, bf16[768,256]{1,0:T(8,128)(2,1)S(1)}, u32[]{:S(2)}) copy-start(bf16[768,256]{1,0:T(8,128)(2,1)S(1)} %get-tuple-element.22.refs_7_) | copy-start | bytes 1179652
  27.8 13.0 %collective-permute-start.12 = (bf16[384,256]{1,0:T(8,128)(2,1)S(1)}, bf16[384,256]{1,0:T(8,128)(2,1)S(1)}, u32[]{:S(2)}, u32[]{:S(2)}) collective-permute-start(bf16[384,256]{1,0:T(8,128)(2,1)S(1)} %get-tuple-element.35), channel_id=1, source_target_pairs={{0,3},{1,0},{2,1},{3,2},{4,7},{5,4},{6,5},{7,6},{8,11},{9,8},{10,9... | collective-permute-start | bytes 589832 | tf_op jit(solution)/shard_map/ppermute | solution.py:515
  40.6 15.7 %collective-permute-start.9 = (bf16[1664,256]{1,0:T(8,128)(2,1)S(1)}, bf16[1664,256]{1,0:T(8,128)(2,1)S(1)}, u32[]{:S(2)}, u32[]{:S(2)}) collective-permute-start(bf16[1664,256]{1,0:T(8,128)(2,1)S(1)} %turn_keys.1.k_ref), channel_id=1, source_target_pairs={{0,4},{4,8},{8,12},{12,16},{16,20},{20,24},{24,28},{28,32},{32,36}... | collective-permute-start | bytes 2555912 | tf_op jit(solution)/shard_map/ppermute | solution.py:515
  40.9 43.7 %copy-start.22 = (bf16[384,1024]{1,0:T(8,128)(2,1)S(1)}, bf16[384,1024]{1,0:T(8,128)(2,1)}, u32[]{:S(2)}) copy-start(bf16[384,1024]{1,0:T(8,128)(2,1)} %param.4) | copy-start | bytes 2359300
  42.0 22.6 %collective-permute-start.13 = (bf16[1536,256]{1,0:T(8,128)(2,1)S(1)}, bf16[1536,256]{1,0:T(8,128)(2,1)S(1)}, u32[]{:S(2)}, u32[]{:S(2)}) collective-permute-start(bf16[1536,256]{1,0:T(8,128)(2,1)S(1)} %assemble.1.v_ref), channel_id=1, source_target_pairs={{0,4},{4,8},{8,12},{12,16},{16,20},{20,24},{24,28},{28,32},{32,36}... | collective-permute-start | bytes 2359304 | tf_op jit(solution)/shard_map/ppermute | solution.py:515
  43.8 20.9 %collective-permute-start.16 = (bf16[1664,256]{1,0:T(8,128)(2,1)S(1)}, bf16[1664,256]{1,0:T(8,128)(2,1)}, u32[]{:S(2)}, u32[]{:S(2)}) collective-permute-start(bf16[1664,256]{1,0:T(8,128)(2,1)S(1)} %turn_keys.1.k_ref), channel_id=1, source_target_pairs={{4,28},{12,4},{20,12},{28,20},{36,60},{44,36},{52,44},{60,52},{68,... | collective-permute-start | bytes 2555912 | tf_op jit(solution)/shard_map/ppermute | solution.py:543
  56.2 17.7 %collective-permute-start.14 = (bf16[1664,256]{1,0:T(8,128)(2,1)S(1)}, bf16[1664,256]{1,0:T(8,128)(2,1)}, u32[]{:S(2)}, u32[]{:S(2)}) collective-permute-start(bf16[1664,256]{1,0:T(8,128)(2,1)S(1)} %collective-permute-done.9.k_ref), channel_id=1, source_target_pairs={{0,4},{4,8},{8,12},{12,16},{16,20},{20,24},{24,28},{28,32},{32,36}... | collective-permute-start | bytes 2555912 | tf_op jit(solution)/shard_map/ppermute | solution.py:515
  56.3 19.9 %collective-permute-start.19 = (bf16[1536,256]{1,0:T(8,128)(2,1)S(1)}, bf16[1536,256]{1,0:T(8,128)(2,1)}, u32[]{:S(2)}, u32[]{:S(2)}) collective-permute-start(bf16[1536,256]{1,0:T(8,128)(2,1)S(1)} %assemble.1.v_ref), channel_id=1, source_target_pairs={{4,28},{12,4},{20,12},{28,20},{36,60},{44,36},{52,44},{60,52},{68,... | collective-permute-start | bytes 2359304 | tf_op jit(solution)/shard_map/ppermute | solution.py:543
  64.7 17.7 %collective-permute-start.15 = (bf16[1536,256]{1,0:T(8,128)(2,1)S(1)}, bf16[1536,256]{1,0:T(8,128)(2,1)}, u32[]{:S(2)}, u32[]{:S(2)}) collective-permute-start(bf16[1536,256]{1,0:T(8,128)(2,1)S(1)} %collective-permute-done.13.v_ref), channel_id=1, source_target_pairs={{0,4},{4,8},{8,12},{12,16},{16,20},{20,24},{24,28},{28,32},{32,36}... | collective-permute-start | bytes 2359304 | tf_op jit(solution)/shard_map/ppermute | solution.py:515
  64.7 72.0 %collective-permute-start.17 = (bf16[1664,256]{1,0:T(8,128)(2,1)}, bf16[1664,256]{1,0:T(8,128)(2,1)}, u32[]{:S(2)}, u32[]{:S(2)}) collective-permute-start(bf16[1664,256]{1,0:T(8,128)(2,1)} %collective-permute-done.16), channel_id=1, source_target_pairs={{28,16},{4,24},{12,32},{20,40},{60,48},{36,56},{44,64},{52,72},{92... | collective-permute-start | bytes 2555912 | tf_op jit(solution)/shard_map/ppermute | solution.py:545
  73.9 62.8 %collective-permute-start.18 = (bf16[1664,256]{1,0:T(8,128)(2,1)}, bf16[1664,256]{1,0:T(8,128)(2,1)}, u32[]{:S(2)}, u32[]{:S(2)}) collective-permute-start(bf16[1664,256]{1,0:T(8,128)(2,1)} %collective-permute-done.14.refs_3_), channel_id=1, source_target_pairs={{0,4},{8,12},{16,20},{24,28},{32,36},{40,44},{48,52},{56,60},{64,6... | collective-permute-start | bytes 2555912 | tf_op jit(solution)/shard_map/ppermute | solution.py:546
  76.1 58.3 %collective-permute-start.20 = (bf16[1536,256]{1,0:T(8,128)(2,1)}, bf16[1536,256]{1,0:T(8,128)(2,1)}, u32[]{:S(2)}, u32[]{:S(2)}) collective-permute-start(bf16[1536,256]{1,0:T(8,128)(2,1)} %collective-permute-done.19), channel_id=1, source_target_pairs={{28,16},{4,24},{12,32},{20,40},{60,48},{36,56},{44,64},{52,72},{92... | collective-permute-start | bytes 2359304 | tf_op jit(solution)/shard_map/ppermute | solution.py:545
  82.3 52.1 %collective-permute-start.21 = (bf16[1536,256]{1,0:T(8,128)(2,1)}, bf16[1536,256]{1,0:T(8,128)(2,1)}, u32[]{:S(2)}, u32[]{:S(2)}) collective-permute-start(bf16[1536,256]{1,0:T(8,128)(2,1)} %collective-permute-done.15.refs_4_), channel_id=1, source_target_pairs={{0,4},{8,12},{16,20},{24,28},{32,36},{40,44},{48,52},{56,60},{64,6... | collective-permute-start | bytes 2359304 | tf_op jit(solution)/shard_map/ppermute | solution.py:546
  85.4 9.0 %collective-permute-start = (bf16[384,256]{1,0:T(8,128)(2,1)S(1)}, bf16[384,256]{1,0:T(8,128)(2,1)S(1)}, u32[]{:S(2)}, u32[]{:S(2)}) collective-permute-start(bf16[384,256]{1,0:T(8,128)(2,1)S(1)} %get-tuple-element.48), channel_id=1, source_target_pairs={{0,1},{1,2},{2,3},{3,0},{4,5},{5,6},{6,7},{7,4},{8,9},{9,10},{10,1... | collective-permute-start | bytes 589832 | tf_op jit(solution)/shard_map/ppermute | solution.py:515
  95.0 7.2 %collective-permute-start.1 = (bf16[384,256]{1,0:T(8,128)(2,1)S(1)}, bf16[384,256]{1,0:T(8,128)(2,1)S(1)}, u32[]{:S(2)}, u32[]{:S(2)}) collective-permute-start(bf16[384,256]{1,0:T(8,128)(2,1)S(1)} %get-tuple-element.50), channel_id=1, source_target_pairs={{0,2},{1,3},{2,0},{3,1},{4,6},{5,7},{6,4},{7,5},{8,10},{9,11},{10,... | collective-permute-start | bytes 589832 | tf_op jit(solution)/shard_map/ppermute | solution.py:515
  102.9 6.0 %collective-permute-start.2 = (bf16[384,256]{1,0:T(8,128)(2,1)}, bf16[384,256]{1,0:T(8,128)(2,1)}, u32[]{:S(2)}, u32[]{:S(2)}) collective-permute-start(bf16[384,256]{1,0:T(8,128)(2,1)} %get-tuple-element.47), channel_id=1, source_target_pairs={{0,3},{1,0},{2,1},{3,2},{4,7},{5,4},{6,5},{7,6},{8,11},{9,8},{10,9... | collective-permute-start | bytes 589832 | tf_op jit(solution)/shard_map/ppermute | solution.py:515
  134.4 4.3 %copy-start.4 = (f32[1536,256]{1,0:T(8,128)}, f32[1536,256]{1,0:T(8,128)S(1)}, u32[]{:S(2)}) copy-start(f32[1536,256]{1,0:T(8,128)S(1)} %get-tuple-element.30.refs_7_) | copy-start | bytes 4718596
  151.7 13.3 %collective-permute-start.22 = (bf16[384,256]{1,0:T(8,128)(2,1)S(1)}, bf16[384,256]{1,0:T(8,128)(2,1)S(1)}, u32[]{:S(2)}, u32[]{:S(2)}) collective-permute-start(bf16[384,256]{1,0:T(8,128)(2,1)S(1)} %get-tuple-element.32), channel_id=1, source_target_pairs={{0,1},{1,2},{2,3},{3,0},{4,5},{5,6},{6,7},{7,4},{8,9},{9,10},{10,1... | collective-permute-start | bytes 589832 | tf_op jit(solution)/shard_map/ppermute | solution.py:515
  151.8 13.2 %collective-permute-start.23 = (bf16[384,256]{1,0:T(8,128)(2,1)S(1)}, bf16[384,256]{1,0:T(8,128)(2,1)S(1)}, u32[]{:S(2)}, u32[]{:S(2)}) collective-permute-start(bf16[384,256]{1,0:T(8,128)(2,1)S(1)} %get-tuple-element.33), channel_id=1, source_target_pairs={{0,2},{1,3},{2,0},{3,1},{4,6},{5,7},{6,4},{7,5},{8,10},{9,11},{10,... | collective-permute-start | bytes 589832 | tf_op jit(solution)/shard_map/ppermute | solution.py:515
  155.9 9.2 %collective-permute-start.24 = (bf16[384,256]{1,0:T(8,128)(2,1)S(1)}, bf16[384,256]{1,0:T(8,128)(2,1)S(1)}, u32[]{:S(2)}, u32[]{:S(2)}) collective-permute-start(bf16[384,256]{1,0:T(8,128)(2,1)S(1)} %get-tuple-element.34), channel_id=1, source_target_pairs={{0,3},{1,0},{2,1},{3,2},{4,7},{5,4},{6,5},{7,6},{8,11},{9,8},{10,9... | collective-permute-start | bytes 589832 | tf_op jit(solution)/shard_map/ppermute | solution.py:515
  (17 other events, 27.3 us)

commit v3 on v2

--- a/solution.py
+++ b/solution.py
@@ -13,7 +13,7 @@
 VMEM = pl.BlockSpec(memory_space=pltpu.VMEM)
 SMEM = pl.BlockSpec(memory_space=pltpu.SMEM)
 GRANT = 24 << 20
-COST = 10**8
+COST = 1000
 
 
 near = pltpu.VMEM
@@ -21,6 +21,10 @@
 
 def keep_near(x):
     return pltpu.with_memory_space_constraint(x, pltpu.VMEM)
+
+
+def keep_far(x):
+    return pltpu.with_memory_space_constraint(x, pltpu.HBM)
 
 
 def dot(a, b):
@@ -56,13 +60,13 @@
     )
 
 
-def put_chunks(here_ref, chunks, out_ref):
+def put_chunks(here_ref, chunks, out_ref, part=None):
     here = here_ref[0]
     parts = len(chunks)
-    rows = chunks[0].shape[0]
+    rows = chunks[0].shape[-2]
     for k, chunk in enumerate(chunks):
         start = pl.multiple_of((here + parts - k) % parts * rows, rows)
-        out_ref[pl.ds(start, rows), :] = chunk[...]
+        out_ref[pl.ds(start, rows), :] = chunk[...] if part is None else chunk[part]
 
 
 def assemble(here, chunks):
@@ -228,7 +232,7 @@
 
 def turn_kernel(here_ref, *refs, group, tail):
     chunks, (w_ref, v0_ref, ft0_ref, v1_ref, ft1_ref, pt_ref, o_ref, x_ref) = refs[:-8], refs[-8:]
-    put_chunks(here_ref, chunks, x_ref)
+    put_chunks(here_ref, chunks, x_ref, 0 if tail else 1)
     length, width = x_ref.shape
     heads = width // DH
     half = length // 2
@@ -263,7 +267,7 @@
         o_ref[length:, :] = pt_ref[...]
 
 
-def turn(here, chunks, w, parts, pt, tail, group=2):
+def turn(here, chunks, w, parts, pt, tail, group=3):
     rows, width = w.shape
     return pl.pallas_call(
         lambda *refs: turn_kernel(*refs, group=group, tail=tail),
@@ -359,8 +363,8 @@
     return pl.pallas_call(
         local_kernel,
         out_shape=(
-            near((rows, width), f32),
-            near((rows, DH), f32),
+            pltpu.HBM((rows, width), f32),
+            pltpu.HBM((rows, DH), f32),
         ),
         in_specs=[VMEM] * 3,
         out_specs=(VMEM,) * 2,
@@ -381,7 +385,9 @@
     return top, acc * keep + both[:, :DH] * gain, total
 
 
-def hop_kernel(ok_ref, z_ref, k_ref, v_ref, acc_ref, stat_ref, out_ref, total_ref, turned_ref, *work):
+def hop_kernel(ok_ref, here_ref, z_ref, k_ref, v_ref, acc_ref, stat_ref, *refs):
+    out_ref, total_ref, turned_ref = refs[:3]
+    own, work = refs[3:6], refs[6:]
     length, width = z_ref.shape
     heads = width // DH
     tiles = length // SPAN
@@ -420,32 +426,43 @@
 
     lax.fori_loop(0, tiles - 1, step, 0)
     one(tiles - 1, False)
-
-
-def attend_hop(ok, z, kp, v, acc, stat):
+    piece = own[0].shape[0]
+    place = pl.ds(pl.multiple_of(here_ref[0] * piece, piece), piece)
+    for source, target in zip((out_ref, total_ref, turned_ref), own):
+        target[...] = source[place, :]
+
+
+def attend_hop(ok, here, z, kp, v, acc, stat, parts):
     rows, width = z.shape
+    shapes = [
+        pltpu.HBM((size, w), kind)
+        for size in (rows, rows // parts)
+        for w, kind in ((width, f32), (DH, f32), (width, bf16))
+    ]
     return pl.pallas_call(
         hop_kernel,
-        out_shape=(near((rows, width), f32), near((rows, DH), f32), near((rows, width), bf16)),
-        in_specs=[SMEM] + [VMEM] * 5,
-        out_specs=(VMEM,) * 3,
+        out_shape=shapes,
+        in_specs=[SMEM] * 2 + [VMEM] * 5,
+        out_specs=(VMEM,) * 6,
         scratch_shapes=scratch(width // DH, rows, SPAN),
         cost_estimate=pl.CostEstimate(flops=COST, bytes_accessed=COST, transcendentals=COST),
         compiler_params=pltpu.CompilerParams(vmem_limit_bytes=GRANT),
         name="attend_hop",
-    )(ok, *map(keep_near, (z, kp, v, acc, stat)))
+    )(ok, here, keep_near(z), keep_near(kp), v, keep_far(acc), keep_far(stat))
 
 
 def last_kernel(ok_ref, here_ref, z_ref, *refs, targets, parts):
     pairs, refs = (refs[:2], refs[2:4]), refs[4:]
     acc_ref, stat_ref, out, work = refs[0], refs[1], refs[2 : 2 + len(targets)], refs[2 + len(targets) :]
     done_ref, turned_ref, work = work[0], work[1], work[2:]
-    length, width = z_ref.shape
+    length, width = pairs[0][1].shape
     heads = width // DH
     piece = length // parts
     order = [(d, h) for d in range(len(pairs)) for h in range(heads)]
 
     def rows_of(i):
+        if z_ref.shape[0] == piece:
+            return slice(None)
         return pl.ds(pl.multiple_of((here_ref[0] + targets[0] + i) % parts * piece, piece), piece)
 
     def first(i, d, h):
@@ -488,11 +505,13 @@
 
 
 def attend_last(ok, here, z, near_pair, far_pair, acc, stat, targets, parts):
-    rows, width = z.shape
+    rows, width = near_pair[1].shape
     piece = rows // parts
     return pl.pallas_call(
         lambda *refs: last_kernel(*refs, targets=targets, parts=parts),
-        out_shape=tuple(near((piece, width), bf16) for _ in targets),
+        out_shape=tuple(
+            (near if len(targets) == 1 else pltpu.HBM)((piece, width), bf16) for _ in targets
+        ),
         in_specs=[SMEM] * 2 + [VMEM] * 7,
         out_specs=(VMEM,) * len(targets),
         scratch_shapes=[
@@ -502,7 +521,7 @@
         + scratch(width // DH, rows, piece),
         cost_estimate=pl.CostEstimate(flops=COST, bytes_accessed=COST, transcendentals=COST),
         compiler_params=pltpu.CompilerParams(vmem_limit_bytes=GRANT),
-    )(ok, here, *map(keep_near, (z, *near_pair, *far_pair, acc, stat)))
+    )(ok, here, keep_far(z), keep_far(near_pair[0]), *map(keep_near, (near_pair[1], *far_pair)), keep_far(acc), keep_far(stat))
 
 
 HOPS = 3
@@ -515,14 +534,18 @@
     return lax.ppermute(value, axis, [(i, (i + by) % length) for i in range(length)])
 
 
-def exchange(array, axis):
+def exchange(*arrays):
     parts = lax.axis_size("head")
     here = lax.axis_index("head")
-    size = array.shape[axis] // parts
-    pieces = [
-        lax.dynamic_slice_in_dim(array, (here + k) % parts * size, size, axis)
-        for k in range(parts)
-    ]
+    size = arrays[0].shape[1] // parts
+
+    def cut(k):
+        found = [
+            lax.dynamic_slice_in_dim(array, (here + k) % parts * size, size, 1) for array in arrays
+        ]
+        return found[0] if len(found) == 1 else jnp.stack(found)
+
+    pieces = [cut(k) for k in range(parts)]
     return pieces[:1] + [shift(piece, "head", k) for k, piece in enumerate(pieces) if k]
 
 
@@ -538,6 +561,14 @@
 
 
 def ring(value):
+    found = []
+    for _ in range(HOPS):
+        value = shift(value, "ctx", 1)
+        found.append(value)
+    return found
+
+
+def relayed(value):
     back, onto, inside = relays(lax.axis_size("ctx"))
     one = shift(value, "ctx", 1)
     passed = lax.ppermute(value, "ctx", back)
@@ -553,24 +584,26 @@
     here = lax.axis_index("head").astype(jnp.int32).reshape(1)
     position = lax.axis_index("ctx")
     oks = [(position >= d).astype(jnp.int32).reshape(1) for d in range(1, HOPS + 1)]
-    w = exchange(directions, 1)
-    v = exchange(values, 1)
-    k = exchange(keys, 1)
-    q = exchange(queries, 1)
+    w = exchange(directions)
+    v = exchange(values)
+    both = exchange(keys, queries)
     v = assemble(here, v)
     low_a, ft_a, w, chain = first_frames(here, w)
     low_b, ft_b, pt = second_frames(w, chain)
     frames = (low_a, ft_a, low_b, ft_b)
-    kp = turn(here, k, w, frames, pt, True)
-    z = turn(here, q, w, frames, pt, False)
+    kp = turn(here, both, w, frames, pt, True)
+    z = turn(here, both, w, frames, pt, False)
     acc, stat = attend_local(z, kp, v)
     vs = ring(v)
-    ks = ring(kp)
-    acc, stat, z = attend_hop(oks[0], z, ks[0], vs[0], acc, stat)
-    state = (jnp.concatenate(oks[1:]), here, z, (ks[1], vs[1]), (ks[2], vs[2]), acc, stat)
-    pieces = attend_last(*state, tuple(range(1, parts)), parts)
+    ks = relayed(kp)
+    acc, stat, z, own_acc, own_stat, own_z = attend_hop(
+        oks[0], here, z, ks[0], vs[0], acc, stat, parts
+    )
+    shared = ((ks[1], vs[1]), (ks[2], vs[2]))
+    ok = jnp.concatenate(oks[1:])
+    pieces = attend_last(ok, here, z, *shared, acc, stat, tuple(range(1, parts)), parts)
     pieces = [shift(piece, "head", k + 1) for k, piece in enumerate(pieces)]
-    pieces = list(attend_last(*state, (0,), parts)) + pieces
+    pieces = list(attend_last(ok, here, own_z, *shared, own_acc, own_stat, (0,), parts)) + pieces
     rows, width = pieces[0].shape
     result = jnp.zeros((rows, width * parts), bf16)
     for k, piece in enumerate(pieces):

time: 167 us -> 159 us (0.952)
  starting transfers between devices: 34.2 us -> 28.5 us
  local copies, waits for them, and re-layouts: 17.2 us -> 13.4 us
    ppermute x6 -> x3, starting transfers between devices: 10.2 us -> 5.1 us  [the longest x1 2.21 us: relayed(): close = lax.ppermute(two, 'ctx', inside)]
    pallas_call x2, Pallas kernels: 13.5 us -> 18.5 us  [the longest x1 12.9 us: attend_hop(): pl.pallas_call(hop_kernel, out_shape=shapes, in_specs=[SMEM] * 2 + [VMEM]...]
    dynamic_slice x4 -> x2, local copies, waits for them, and re-layouts: 3.13 us -> 0.22 us  [cut(): lax.dynamic_slice_in_dim(array, (here + k) % parts * size, size, 1)]
    pallas_call x2 -> x1, Pallas kernels: 4.22 us -> 1.7 us  [pick(): pl.pallas_call(pick_kernel, out_shape=near(one.shape, one.dtype), in_spec...]
    pallas_call x2, Pallas kernels: 8.51 us -> 6.06 us  [turn(): pl.pallas_call(lambda *refs: turn_kernel(*refs, group=group, tail=tail),...]
    unnamed x48 -> x42, local copies, waits for them, and re-layouts: 13.2 us -> 10.8 us
    pallas_call x2, Pallas kernels: 18.2 us -> 20.5 us  [attend_last(): pl.pallas_call(lambda *refs: last_kernel(*refs, targets=targets, parts=pa...]
    ppermute x19 -> x17, starting transfers between devices: 24.1 us -> 23.4 us  [shift(): lax.ppermute(value, axis, [(i, (i + by) % length) for i in range(length)])]
  transfers between devices with their start and end apart: 25 -> 20, of which waited for: 9 -> 10; matrix products, arithmetic and copies ran while one was open for 1% -> 0% of each run, Pallas kernels for 27% -> 29%
where the time goes in v3:
time: 159 us
  Pallas kernels  61.6 us (39%)
  waiting for transfers between devices  54.8 us (34%)
  starting transfers between devices  28.5 us (18%)
  local copies, waits for them, and re-layouts  13.4 us (8%)
    ppermute x17, waiting for transfers between devices, shift(): lax.ppermute(value, axis, [(i, (i + by) % length) for i in range(length)])  54.8 us
    ppermute x17, starting transfers between devices, shift(): lax.ppermute(value, axis, [(i, (i + by) % length) for i in range(length)])  23.4 us
    pallas_call x2, Pallas kernels, attend_last(): pl.pallas_call(lambda *refs: last_kernel(*refs, targets=targets, parts=pa...  20.5 us
    pallas_call x1, Pallas kernels, attend_hop(): pl.pallas_call(hop_kernel, out_shape=shapes, in_specs=[SMEM] * 2 + [VMEM]...  12.9 us
    unnamed x42, local copies, waits for them, and re-layouts  10.8 us
    pallas_call x1, Pallas kernels, first_frames(): pl.pallas_call(lambda *refs: frames_kernel(*refs, group=group, first=True...  7.47 us
    pallas_call x1, Pallas kernels, second_frames(): pl.pallas_call(lambda *refs: frames_kernel(*refs, group=group, first=Fals...  7.42 us
    pallas_call x2, Pallas kernels, turn(): pl.pallas_call(lambda *refs: turn_kernel(*refs, group=group, tail=tail),...  6.06 us
  transfers between devices with their start and end apart: 20, of which 10 were waited for; matrix products, arithmetic and copies ran while one was open for 0% of the time, Pallas kernels for 29%

profile of v3, /device:TPU:0, one launch (start us, length us, event | category | flops | bytes accessed | tf_op | source)
XLA Modules:
  0.0 158.9 jit_solution(15414944308401644619)
XLA Ops:
  0.0 1.6 dynamic-slice_bitcast_fusion
  1.6 2.1 %collective-permute-start = (bf16[2,384,256]{2,1,0:T(8,128)(2,1)S(1)}, bf16[2,384,256]{2,1,0:T(8,128)(2,1)S(1)}, u32[]{:S(2)}, u32[]{:S(2)}) collective-permute-start(bf16[2,384,256]{2,1,0:T(8,128)(2,1)S(1)} %pad_maximum_fusion.1), channel_id=1, source_target_pairs={{0,1},{1,2},{2,3},{3,0},{4,5},{5,6},{6,7},{7,4},{8,9},{9,10},{10,1... | collective-permute-start | bytes 1179656 | tf_op jit(solution)/shard_map/ppermute | solution.py:534
  3.8 3.7 %collective-permute-start.1 = (bf16[2,384,256]{2,1,0:T(8,128)(2,1)S(1)}, bf16[2,384,256]{2,1,0:T(8,128)(2,1)S(1)}, u32[]{:S(2)}, u32[]{:S(2)}) collective-permute-start(bf16[2,384,256]{2,1,0:T(8,128)(2,1)S(1)} %pad_maximum_fusion.2), channel_id=1, source_target_pairs={{0,2},{1,3},{2,0},{3,1},{4,6},{5,7},{6,4},{7,5},{8,10},{9,11},{10,... | collective-permute-start | bytes 1179656 | tf_op jit(solution)/shard_map/ppermute | solution.py:534
  7.7 3.3 %collective-permute-start.2 = (bf16[2,384,256]{2,1,0:T(8,128)(2,1)S(1)}, bf16[2,384,256]{2,1,0:T(8,128)(2,1)S(1)}, u32[]{:S(2)}, u32[]{:S(2)}) collective-permute-start(bf16[2,384,256]{2,1,0:T(8,128)(2,1)S(1)} %pad_maximum_fusion.3), channel_id=1, source_target_pairs={{0,3},{1,0},{2,1},{3,2},{4,7},{5,4},{6,5},{7,6},{8,11},{9,8},{10,9... | collective-permute-start | bytes 1179656 | tf_op jit(solution)/shard_map/ppermute | solution.py:534
  11.0 16.6 %collective-permute-done.3.refs_2_ = bf16[384,256]{1,0:T(8,128)(2,1)S(1)} collective-permute-done((bf16[384,256]{1,0:T(8,128)(2,1)S(1)}, bf16[384,256]{1,0:T(8,128)(2,1)S(1)}, u32[]{:S(2)}, u32[]{:S(2)}) %collective-permute-start.3) | collective-permute-done | bytes 196640 | tf_op jit(solution)/shard_map/ppermute | solution.py:534
  27.6 2.9 %collective-permute-start.5 = (bf16[384,256]{1,0:T(8,128)(2,1)S(1)}, bf16[384,256]{1,0:T(8,128)(2,1)S(1)}, u32[]{:S(2)}, u32[]{:S(2)}) collective-permute-start(bf16[384,256]{1,0:T(8,128)(2,1)S(1)} %get-tuple-element.45), channel_id=1, source_target_pairs={{0,3},{1,0},{2,1},{3,2},{4,7},{5,4},{6,5},{7,6},{8,11},{9,8},{10,9... | collective-permute-start | bytes 589832 | tf_op jit(solution)/shard_map/ppermute | solution.py:534
  30.7 2.5 %collective-permute-done.4.refs_3_ = bf16[384,256]{1,0:T(8,128)(2,1)S(1)} collective-permute-done((bf16[384,256]{1,0:T(8,128)(2,1)S(1)}, bf16[384,256]{1,0:T(8,128)(2,1)S(1)}, u32[]{:S(2)}, u32[]{:S(2)}) %collective-permute-start.4) | collective-permute-done | bytes 196640 | tf_op jit(solution)/shard_map/ppermute | solution.py:534
  33.2 1.3 collective-permute-done.5.refs_4_
  34.6 6.3 %collective-permute-start.8 = (bf16[384,256]{1,0:T(8,128)(2,1)S(1)}, bf16[384,256]{1,0:T(8,128)(2,1)S(1)}, u32[]{:S(2)}, u32[]{:S(2)}) collective-permute-start(bf16[384,256]{1,0:T(8,128)(2,1)S(1)} %get-tuple-element.44), channel_id=1, source_target_pairs={{0,2},{1,3},{2,0},{3,1},{4,6},{5,7},{6,4},{7,5},{8,10},{9,11},{10,... | collective-permute-start | bytes 589832 | tf_op jit(solution)/shard_map/ppermute | solution.py:534
  40.9 7.5 %first_frames.1 = (f32[768,256]{1,0:T(8,128)S(1)}, bf16[768,256]{1,0:T(8,128)(2,1)S(1)}, bf16[1536,256]{1,0:T(8,128)(2,1)S(1)}, f32[2,128,128]{2,1,0:T(8,128)S(1)}) custom-call(s32[1]{0:T(128)} %bitcast.2.refs_0_.here_ref.refs_1_, bf16[384,256]{1,0:T(8,128)(2,1)S(1)} %get-tuple-element.47.refs_1_, bf16[384,256]{1,0:T(8,128)(2,1)S(1)} %collective-permute-done.3.refs_2_, ...), custom_call_target="tpu_custom_call" | custom-call | flops 1000 | bytes 1000 | tf_op jit(solution)/shard_map/first_frames/pallas_call | solution.py:198
  48.4 7.4 %second_frames.1 = (f32[768,256]{1,0:T(8,128)S(1)}, bf16[768,256]{1,0:T(8,128)(2,1)S(1)}, bf16[128,256]{1,0:T(8,128)(2,1)S(1)}) custom-call(bf16[1536,256]{1,0:T(8,128)(2,1)S(1)} %get-tuple-element.23.refs_0_.refs_5_, f32[2,128,128]{2,1,0:T(8,128)S(1)} %get-tuple-element.26.refs_1_), custom_call_target="tpu_custom_call" | custom-call | flops 1000 | bytes 1000 | tf_op jit(solution)/shard_map/second_frames/pallas_call | solution.py:217
  56.1 3.0 %turn_keys.1.k_ref = bf16[1664,256]{1,0:T(8,128)(2,1)S(1)} custom-call(s32[1]{0:T(128)} %bitcast.2.refs_0_.here_ref.refs_1_, bf16[2,384,256]{2,1,0:T(8,128)(2,1)S(1)} %pad_maximum_fusion.refs_1_, bf16[2,384,256]{2,1,0:T(8,128)(2,1)S(1)} %collective-permute-done.refs_2_, bf16[2,384,256]{2,1,0:T(8,128)(2,1)S(1)} %collective-permute-done.1.refs_3_, ...), custom_call_target="tpu_custom_call" | custom-call | flops 1000 | bytes 1000 | tf_op jit(solution)/shard_map/turn_keys/pallas_call | solution.py:272
  59.3 2.4 %collective-permute-done.9.refs_3_ = bf16[384,256]{1,0:T(8,128)(2,1)S(1)} collective-permute-done((bf16[384,256]{1,0:T(8,128)(2,1)S(1)}, bf16[384,256]{1,0:T(8,128)(2,1)S(1)}, u32[]{:S(2)}, u32[]{:S(2)}) %collective-permute-start.9) | collective-permute-done | bytes 196640 | tf_op jit(solution)/shard_map/ppermute | solution.py:534
  62.8 1.6 %collective-permute-start.13 = (bf16[1664,256]{1,0:T(8,128)(2,1)S(1)}, bf16[1664,256]{1,0:T(8,128)(2,1)}, u32[]{:S(2)}, u32[]{:S(2)}) collective-permute-start(bf16[1664,256]{1,0:T(8,128)(2,1)S(1)} %turn_keys.1.k_ref), channel_id=1, source_target_pairs={{4,28},{12,4},{20,12},{28,20},{36,60},{44,36},{52,44},{60,52},{68,... | collective-permute-start | bytes 2555912 | tf_op jit(solution)/shard_map/ppermute | solution.py:574
  64.4 10.3 %collective-permute-done.6.k_ref = bf16[1664,256]{1,0:T(8,128)(2,1)S(1)} collective-permute-done((bf16[1664,256]{1,0:T(8,128)(2,1)S(1)}, bf16[1664,256]{1,0:T(8,128)(2,1)S(1)}, u32[]{:S(2)}, u32[]{:S(2)}) %collective-permute-start.6) | collective-permute-done | bytes 852000 | tf_op jit(solution)/shard_map/ppermute | solution.py:534
  75.6 7.5 %collective-permute-done.10.v_ref = bf16[1536,256]{1,0:T(8,128)(2,1)S(1)} collective-permute-done((bf16[1536,256]{1,0:T(8,128)(2,1)S(1)}, bf16[1536,256]{1,0:T(8,128)(2,1)S(1)}, u32[]{:S(2)}, u32[]{:S(2)}) %collective-permute-start.10) | collective-permute-done | bytes 786464 | tf_op jit(solution)/shard_map/ppermute | solution.py:534
  84.1 1.3 collective-permute-start.14
  85.4 7.0 %collective-permute-done.11.refs_3_ = bf16[1664,256]{1,0:T(8,128)(2,1)} collective-permute-done((bf16[1664,256]{1,0:T(8,128)(2,1)S(1)}, bf16[1664,256]{1,0:T(8,128)(2,1)}, u32[]{:S(2)}, u32[]{:S(2)}) %collective-permute-start.11) | collective-permute-done | bytes 852000 | tf_op jit(solution)/shard_map/ppermute | solution.py:534
  92.4 2.2 %collective-permute-start.15 = (bf16[1664,256]{1,0:T(8,128)(2,1)}, bf16[1664,256]{1,0:T(8,128)(2,1)}, u32[]{:S(2)}, u32[]{:S(2)}) collective-permute-start(bf16[1664,256]{1,0:T(8,128)(2,1)} %collective-permute-done.11.refs_3_), channel_id=1, source_target_pairs={{0,4},{8,12},{16,20},{24,28},{32,36},{40,44},{48,52},{56,60},{64,6... | collective-permute-start | bytes 2555912 | tf_op jit(solution)/shard_map/ppermute | solution.py:577
  94.6 6.2 %collective-permute-done.12.refs_4_ = bf16[1536,256]{1,0:T(8,128)(2,1)} collective-permute-done((bf16[1536,256]{1,0:T(8,128)(2,1)S(1)}, bf16[1536,256]{1,0:T(8,128)(2,1)}, u32[]{:S(2)}, u32[]{:S(2)}) %collective-permute-start.12) | collective-permute-done | bytes 786464 | tf_op jit(solution)/shard_map/ppermute | solution.py:534
  100.9 1.1 copy-done.3
  102.0 1.1 copy-done.5
  104.1 1.0 copy-done.9
  107.1 3.0 %turn_queries.1.q_ref.z_ref = bf16[1536,256]{1,0:T(8,128)(2,1)S(1)} custom-call(s32[1]{0:T(128)} %bitcast.2.refs_0_.here_ref.refs_1_, bf16[2,384,256]{2,1,0:T(8,128)(2,1)S(1)} %pad_maximum_fusion.refs_1_, bf16[2,384,256]{2,1,0:T(8,128)(2,1)S(1)} %collective-permute-done.refs_2_, bf16[2,384,256]{2,1,0:T(8,128)(2,1)S(1)} %copy-done.7, ...), custom_call_target="tpu_custom_call" | custom-call | flops 1000 | bytes 1000 | tf_op jit(solution)/shard_map/turn_queries/pallas_call | solution.py:272
  110.2 1.1 copy-done.1
  111.3 5.6 %attend_local.1 = (f32[1536,256]{1,0:T(8,128)}, f32[1536,128]{1,0:T(8,128)}) custom-call(bf16[1536,256]{1,0:T(8,128)(2,1)S(1)} %turn_queries.1.q_ref.z_ref, bf16[1664,256]{1,0:T(8,128)(2,1)S(1)} %turn_keys.1.k_ref, bf16[1536,256]{1,0:T(8,128)(2,1)S(1)} %copy-done.1), custom_call_target="tpu_custom_call" | custom-call | flops 1000 | bytes 1000 | tf_op jit(solution)/shard_map/attend_local/pallas_call | solution.py:363
  116.9 12.9 %attend_hop.1 = (f32[1536,256]{1,0:T(8,128)}, f32[1536,128]{1,0:T(8,128)}, bf16[1536,256]{1,0:T(8,128)(2,1)}, f32[384,256]{1,0:T(8,128)}, f32[384,128]{1,0:T(8,128)}, /*index=5*/bf16[384,256]{1,0:T(8,128)(2,1)}) custom-call(s32[1]{0:T(128)} %bitcast.3.ok_ref, s32[1]{0:T(128)} %bitcast.2.refs_0_.here_ref.refs_1_, ...), custom_call_target="tpu_custom_call" | custom-call | flops 1000 | bytes 1000 | tf_op jit(solution)/shard_map/attend_hop/pallas_call | solution.py:442
  129.8 1.7 %pick.1.refs_5_ = bf16[1664,256]{1,0:T(8,128)(2,1)S(1)} custom-call(s32[1]{0:T(128)} %bitcast.12.first_ref, bf16[1664,256]{1,0:T(8,128)(2,1)} %collective-permute-done.14.one_ref, bf16[1664,256]{1,0:T(8,128)(2,1)} %collective-permute-done.15.two_ref), custom_call_target="tpu_custom_call" | custom-call | flops 1000 | bytes 1000 | tf_op jit(solution)/shard_map/pick/pallas_call | solution.py:96
  131.5 14.8 %shard_map.47 = (bf16[384,256]{1,0:T(8,128)(2,1)}, bf16[384,256]{1,0:T(8,128)(2,1)}, bf16[384,256]{1,0:T(8,128)(2,1)}) custom-call(s32[2]{0:T(128)S(1)} %add_convert_fusion.refs_0_, s32[1]{0:T(128)} %bitcast.2.refs_0_.here_ref.refs_1_, bf16[1536,256]{1,0:T(8,128)(2,1)} %get-tuple-element.35.refs_2_, bf16[1664,256]{1,0:T(8,128)(2,1)} %collective-permute-done.11.refs_3_, ...), custom_call_target="tpu_custom_call" | custom-call | flops 1000 | bytes 1000 | tf_op jit(solution)/shard_map/pallas_call | solution.py:510
  146.3 2.0 %collective-permute-start.17 = (bf16[384,256]{1,0:T(8,128)(2,1)}, bf16[384,256]{1,0:T(8,128)(2,1)S(1)}, u32[]{:S(2)}, u32[]{:S(2)}) collective-permute-start(bf16[384,256]{1,0:T(8,128)(2,1)} %get-tuple-element.38), channel_id=1, source_target_pairs={{0,1},{1,2},{2,3},{3,0},{4,5},{5,6},{6,7},{7,4},{8,9},{9,10},{10,1... | collective-permute-start | bytes 589832 | tf_op jit(solution)/shard_map/ppermute | solution.py:534
  148.3 2.7 %collective-permute-start.19 = (bf16[384,256]{1,0:T(8,128)(2,1)}, bf16[384,256]{1,0:T(8,128)(2,1)S(1)}, u32[]{:S(2)}, u32[]{:S(2)}) collective-permute-start(bf16[384,256]{1,0:T(8,128)(2,1)} %get-tuple-element.40), channel_id=1, source_target_pairs={{0,3},{1,0},{2,1},{3,2},{4,7},{5,4},{6,5},{7,6},{8,11},{9,8},{10,9... | collective-permute-start | bytes 589832 | tf_op jit(solution)/shard_map/ppermute | solution.py:534
  151.0 5.6 %shard_map.46 = bf16[384,256]{1,0:T(8,128)(2,1)S(1)} custom-call(s32[2]{0:T(128)S(1)} %add_convert_fusion.refs_0_, s32[1]{0:T(128)} %bitcast.2.refs_0_.here_ref.refs_1_, bf16[384,256]{1,0:T(8,128)(2,1)} %get-tuple-element.32.refs_2_, bf16[1664,256]{1,0:T(8,128)(2,1)} %collective-permute-done.11.refs_3_, bf16[1536,256]{1,0:T(8,128)(2,1)} %collective-permute-done.12.refs_4_, ...), custom_call_target="tpu_custom_call" | custom-call | flops 1000 | bytes 1000 | tf_op jit(solution)/shard_map/pallas_call | solution.py:510
  (73 shorter events, 9.1 us)
Async XLA Ops:
  1.6 5.9 %copy-start.18 = (bf16[384,1024]{1,0:T(8,128)(2,1)S(1)}, bf16[384,1024]{1,0:T(8,128)(2,1)}, u32[]{:S(2)}) copy-start(bf16[384,1024]{1,0:T(8,128)(2,1)} %param.7) | copy-start | bytes 2359300
  1.6 54.2 %collective-permute-start = (bf16[2,384,256]{2,1,0:T(8,128)(2,1)S(1)}, bf16[2,384,256]{2,1,0:T(8,128)(2,1)S(1)}, u32[]{:S(2)}, u32[]{:S(2)}) collective-permute-start(bf16[2,384,256]{2,1,0:T(8,128)(2,1)S(1)} %pad_maximum_fusion.1), channel_id=1, source_target_pairs={{0,1},{1,2},{2,3},{3,0},{4,5},{5,6},{6,7},{7,4},{8,9},{9,10},{10,1... | collective-permute-start | bytes 1179656 | tf_op jit(solution)/shard_map/ppermute | solution.py:534
  3.8 26.8 %copy-start.19 = (bf16[384,1024]{1,0:T(8,128)(2,1)S(1)}, bf16[384,1024]{1,0:T(8,128)(2,1)}, u32[]{:S(2)}) copy-start(bf16[384,1024]{1,0:T(8,128)(2,1)} %param.6) | copy-start | bytes 2359300
  3.8 52.3 %collective-permute-start.1 = (bf16[2,384,256]{2,1,0:T(8,128)(2,1)S(1)}, bf16[2,384,256]{2,1,0:T(8,128)(2,1)S(1)}, u32[]{:S(2)}, u32[]{:S(2)}) collective-permute-start(bf16[2,384,256]{2,1,0:T(8,128)(2,1)S(1)} %pad_maximum_fusion.2), channel_id=1, source_target_pairs={{0,2},{1,3},{2,0},{3,1},{4,6},{5,7},{6,4},{7,5},{8,10},{9,11},{10,... | collective-permute-start | bytes 1179656 | tf_op jit(solution)/shard_map/ppermute | solution.py:534
  7.6 20.1 %collective-permute-start.3 = (bf16[384,256]{1,0:T(8,128)(2,1)S(1)}, bf16[384,256]{1,0:T(8,128)(2,1)S(1)}, u32[]{:S(2)}, u32[]{:S(2)}) collective-permute-start(bf16[384,256]{1,0:T(8,128)(2,1)S(1)} %get-tuple-element.46), channel_id=1, source_target_pairs={{0,1},{1,2},{2,3},{3,0},{4,5},{5,6},{6,7},{7,4},{8,9},{9,10},{10,1... | collective-permute-start | bytes 589832 | tf_op jit(solution)/shard_map/ppermute | solution.py:534
  7.7 48.4 %collective-permute-start.2 = (bf16[2,384,256]{2,1,0:T(8,128)(2,1)S(1)}, bf16[2,384,256]{2,1,0:T(8,128)(2,1)S(1)}, u32[]{:S(2)}, u32[]{:S(2)}) collective-permute-start(bf16[2,384,256]{2,1,0:T(8,128)(2,1)S(1)} %pad_maximum_fusion.3), channel_id=1, source_target_pairs={{0,3},{1,0},{2,1},{3,2},{4,7},{5,4},{6,5},{7,6},{8,11},{9,8},{10,9... | collective-permute-start | bytes 1179656 | tf_op jit(solution)/shard_map/ppermute | solution.py:534
  11.0 22.2 %collective-permute-start.4 = (bf16[384,256]{1,0:T(8,128)(2,1)S(1)}, bf16[384,256]{1,0:T(8,128)(2,1)S(1)}, u32[]{:S(2)}, u32[]{:S(2)}) collective-permute-start(bf16[384,256]{1,0:T(8,128)(2,1)S(1)} %get-tuple-element.48), channel_id=1, source_target_pairs={{0,2},{1,3},{2,0},{3,1},{4,6},{5,7},{6,4},{7,5},{8,10},{9,11},{10,... | collective-permute-start | bytes 589832 | tf_op jit(solution)/shard_map/ppermute | solution.py:534
  27.6 7.0 %collective-permute-start.5 = (bf16[384,256]{1,0:T(8,128)(2,1)S(1)}, bf16[384,256]{1,0:T(8,128)(2,1)S(1)}, u32[]{:S(2)}, u32[]{:S(2)}) collective-permute-start(bf16[384,256]{1,0:T(8,128)(2,1)S(1)} %get-tuple-element.45), channel_id=1, source_target_pairs={{0,3},{1,0},{2,1},{3,2},{4,7},{5,4},{6,5},{7,6},{8,11},{9,8},{10,9... | collective-permute-start | bytes 589832 | tf_op jit(solution)/shard_map/ppermute | solution.py:534
  33.2 26.1 %collective-permute-start.7 = (bf16[384,256]{1,0:T(8,128)(2,1)S(1)}, bf16[384,256]{1,0:T(8,128)(2,1)S(1)}, u32[]{:S(2)}, u32[]{:S(2)}) collective-permute-start(bf16[384,256]{1,0:T(8,128)(2,1)S(1)} %get-tuple-element.42), channel_id=1, source_target_pairs={{0,1},{1,2},{2,3},{3,0},{4,5},{5,6},{6,7},{7,4},{8,9},{9,10},{10,1... | collective-permute-start | bytes 589832 | tf_op jit(solution)/shard_map/ppermute | solution.py:534
  34.6 24.7 %collective-permute-start.8 = (bf16[384,256]{1,0:T(8,128)(2,1)S(1)}, bf16[384,256]{1,0:T(8,128)(2,1)S(1)}, u32[]{:S(2)}, u32[]{:S(2)}) collective-permute-start(bf16[384,256]{1,0:T(8,128)(2,1)S(1)} %get-tuple-element.44), channel_id=1, source_target_pairs={{0,2},{1,3},{2,0},{3,1},{4,6},{5,7},{6,4},{7,5},{8,10},{9,11},{10,... | collective-permute-start | bytes 589832 | tf_op jit(solution)/shard_map/ppermute | solution.py:534
  48.3 10.8 %copy-start.2 = (f32[768,256]{1,0:T(8,128)}, f32[768,256]{1,0:T(8,128)S(1)}, u32[]{:S(2)}) copy-start(f32[768,256]{1,0:T(8,128)S(1)} %get-tuple-element.24.refs_6_) | copy-start | bytes 2359300
  48.3 10.8 %copy-start.10 = (bf16[768,256]{1,0:T(8,128)(2,1)}, bf16[768,256]{1,0:T(8,128)(2,1)S(1)}, u32[]{:S(2)}) copy-start(bf16[768,256]{1,0:T(8,128)(2,1)S(1)} %get-tuple-element.25.refs_7_) | copy-start | bytes 1179652
  55.8 3.4 %copy-start.4 = (f32[768,256]{1,0:T(8,128)}, f32[768,256]{1,0:T(8,128)S(1)}, u32[]{:S(2)}) copy-start(f32[768,256]{1,0:T(8,128)S(1)} %get-tuple-element.27.refs_8_) | copy-start | bytes 2359300
  55.8 3.4 %copy-start.12 = (bf16[768,256]{1,0:T(8,128)(2,1)}, bf16[768,256]{1,0:T(8,128)(2,1)S(1)}, u32[]{:S(2)}) copy-start(bf16[768,256]{1,0:T(8,128)(2,1)S(1)} %get-tuple-element.28.refs_9_) | copy-start | bytes 1179652
  55.8 5.9 %collective-permute-start.9 = (bf16[384,256]{1,0:T(8,128)(2,1)S(1)}, bf16[384,256]{1,0:T(8,128)(2,1)S(1)}, u32[]{:S(2)}, u32[]{:S(2)}) collective-permute-start(bf16[384,256]{1,0:T(8,128)(2,1)S(1)} %get-tuple-element.41), channel_id=1, source_target_pairs={{0,3},{1,0},{2,1},{3,2},{4,7},{5,4},{6,5},{7,6},{8,11},{9,8},{10,9... | collective-permute-start | bytes 589832 | tf_op jit(solution)/shard_map/ppermute | solution.py:534
  56.1 3.1 %copy-start.6 = (bf16[2,384,256]{2,1,0:T(8,128)(2,1)}, bf16[2,384,256]{2,1,0:T(8,128)(2,1)S(1)}, u32[]{:S(2)}) copy-start(bf16[2,384,256]{2,1,0:T(8,128)(2,1)S(1)} %collective-permute-done.1.refs_3_) | copy-start | bytes 1179652
  56.1 3.1 %copy-start.8 = (bf16[2,384,256]{2,1,0:T(8,128)(2,1)}, bf16[2,384,256]{2,1,0:T(8,128)(2,1)S(1)}, u32[]{:S(2)}) copy-start(bf16[2,384,256]{2,1,0:T(8,128)(2,1)S(1)} %collective-permute-done.2.refs_4_) | copy-start | bytes 1179652
  59.2 15.5 %collective-permute-start.6 = (bf16[1664,256]{1,0:T(8,128)(2,1)S(1)}, bf16[1664,256]{1,0:T(8,128)(2,1)S(1)}, u32[]{:S(2)}, u32[]{:S(2)}) collective-permute-start(bf16[1664,256]{1,0:T(8,128)(2,1)S(1)} %turn_keys.1.k_ref), channel_id=1, source_target_pairs={{0,4},{4,8},{8,12},{12,16},{16,20},{20,24},{24,28},{28,32},{32,36}... | collective-permute-start | bytes 2555912 | tf_op jit(solution)/shard_map/ppermute | solution.py:534
  61.8 21.4 %collective-permute-start.10 = (bf16[1536,256]{1,0:T(8,128)(2,1)S(1)}, bf16[1536,256]{1,0:T(8,128)(2,1)S(1)}, u32[]{:S(2)}, u32[]{:S(2)}) collective-permute-start(bf16[1536,256]{1,0:T(8,128)(2,1)S(1)} %assemble.1.v_ref), channel_id=1, source_target_pairs={{0,4},{4,8},{8,12},{12,16},{16,20},{20,24},{24,28},{28,32},{32,36}... | collective-permute-start | bytes 2359304 | tf_op jit(solution)/shard_map/ppermute | solution.py:534
  62.8 21.3 %collective-permute-start.13 = (bf16[1664,256]{1,0:T(8,128)(2,1)S(1)}, bf16[1664,256]{1,0:T(8,128)(2,1)}, u32[]{:S(2)}, u32[]{:S(2)}) collective-permute-start(bf16[1664,256]{1,0:T(8,128)(2,1)S(1)} %turn_keys.1.k_ref), channel_id=1, source_target_pairs={{4,28},{12,4},{20,12},{28,20},{36,60},{44,36},{52,44},{60,52},{68,... | collective-permute-start | bytes 2555912 | tf_op jit(solution)/shard_map/ppermute | solution.py:574
  74.7 17.7 %collective-permute-start.11 = (bf16[1664,256]{1,0:T(8,128)(2,1)S(1)}, bf16[1664,256]{1,0:T(8,128)(2,1)}, u32[]{:S(2)}, u32[]{:S(2)}) collective-permute-start(bf16[1664,256]{1,0:T(8,128)(2,1)S(1)} %collective-permute-done.6.k_ref), channel_id=1, source_target_pairs={{0,4},{4,8},{8,12},{12,16},{16,20},{20,24},{24,28},{28,32},{32,36}... | collective-permute-start | bytes 2555912 | tf_op jit(solution)/shard_map/ppermute | solution.py:534
  83.1 17.7 %collective-permute-start.12 = (bf16[1536,256]{1,0:T(8,128)(2,1)S(1)}, bf16[1536,256]{1,0:T(8,128)(2,1)}, u32[]{:S(2)}, u32[]{:S(2)}) collective-permute-start(bf16[1536,256]{1,0:T(8,128)(2,1)S(1)} %collective-permute-done.10.v_ref), channel_id=1, source_target_pairs={{0,4},{4,8},{8,12},{12,16},{16,20},{20,24},{24,28},{28,32},{32,36}... | collective-permute-start | bytes 2359304 | tf_op jit(solution)/shard_map/ppermute | solution.py:534
  84.1 45.7 %collective-permute-start.14 = (bf16[1664,256]{1,0:T(8,128)(2,1)}, bf16[1664,256]{1,0:T(8,128)(2,1)}, u32[]{:S(2)}, u32[]{:S(2)}) collective-permute-start(bf16[1664,256]{1,0:T(8,128)(2,1)} %collective-permute-done.13), channel_id=1, source_target_pairs={{28,16},{4,24},{12,32},{20,40},{60,48},{36,56},{44,64},{52,72},{92... | collective-permute-start | bytes 2555912 | tf_op jit(solution)/shard_map/ppermute | solution.py:576
  92.4 37.4 %collective-permute-start.15 = (bf16[1664,256]{1,0:T(8,128)(2,1)}, bf16[1664,256]{1,0:T(8,128)(2,1)}, u32[]{:S(2)}, u32[]{:S(2)}) collective-permute-start(bf16[1664,256]{1,0:T(8,128)(2,1)} %collective-permute-done.11.refs_3_), channel_id=1, source_target_pairs={{0,4},{8,12},{16,20},{24,28},{32,36},{40,44},{48,52},{56,60},{64,6... | collective-permute-start | bytes 2555912 | tf_op jit(solution)/shard_map/ppermute | solution.py:577
  100.8 30.7 %collective-permute-start.16 = (bf16[1536,256]{1,0:T(8,128)(2,1)}, bf16[1536,256]{1,0:T(8,128)(2,1)}, u32[]{:S(2)}, u32[]{:S(2)}) collective-permute-start(bf16[1536,256]{1,0:T(8,128)(2,1)} %collective-permute-done.12.refs_4_), channel_id=1, source_target_pairs={{0,4},{4,8},{8,12},{12,16},{16,20},{20,24},{24,28},{28,32},{32,36}... | collective-permute-start | bytes 2359304 | tf_op jit(solution)/shard_map/ppermute | solution.py:534
  100.9 1.1 copy-start.3
  110.2 1.1 copy-start.1
  111.3 5.6 %copy-start.15 = (bf16[1664,256]{1,0:T(8,128)(2,1)S(1)}, bf16[1664,256]{1,0:T(8,128)(2,1)}, u32[]{:S(2)}) copy-start(bf16[1664,256]{1,0:T(8,128)(2,1)} %copy-done.14) | copy-start | bytes 2555908
  111.3 5.6 %copy-start.17 = (bf16[1536,256]{1,0:T(8,128)(2,1)S(1)}, bf16[1536,256]{1,0:T(8,128)(2,1)}, u32[]{:S(2)}) copy-start(bf16[1536,256]{1,0:T(8,128)(2,1)} %copy-done.16) | copy-start | bytes 2359300
  146.3 11.0 %collective-permute-start.17 = (bf16[384,256]{1,0:T(8,128)(2,1)}, bf16[384,256]{1,0:T(8,128)(2,1)S(1)}, u32[]{:S(2)}, u32[]{:S(2)}) collective-permute-start(bf16[384,256]{1,0:T(8,128)(2,1)} %get-tuple-element.38), channel_id=1, source_target_pairs={{0,1},{1,2},{2,3},{3,0},{4,5},{5,6},{6,7},{7,4},{8,9},{9,10},{10,1... | collective-permute-start | bytes 589832 | tf_op jit(solution)/shard_map/ppermute | solution.py:534
  148.3 9.0 %collective-permute-start.18 = (bf16[384,256]{1,0:T(8,128)(2,1)}, bf16[384,256]{1,0:T(8,128)(2,1)S(1)}, u32[]{:S(2)}, u32[]{:S(2)}) collective-permute-start(bf16[384,256]{1,0:T(8,128)(2,1)} %get-tuple-element.39), channel_id=1, source_target_pairs={{0,2},{1,3},{2,0},{3,1},{4,6},{5,7},{6,4},{7,5},{8,10},{9,11},{10,... | collective-permute-start | bytes 589832 | tf_op jit(solution)/shard_map/ppermute | solution.py:534
  148.3 9.4 %collective-permute-start.19 = (bf16[384,256]{1,0:T(8,128)(2,1)}, bf16[384,256]{1,0:T(8,128)(2,1)S(1)}, u32[]{:S(2)}, u32[]{:S(2)}) collective-permute-start(bf16[384,256]{1,0:T(8,128)(2,1)} %get-tuple-element.40), channel_id=1, source_target_pairs={{0,3},{1,0},{2,1},{3,2},{4,7},{5,4},{6,5},{7,6},{8,11},{9,8},{10,9... | collective-permute-start | bytes 589832 | tf_op jit(solution)/shard_map/ppermute | solution.py:534
  (9 other events, 8.8 us)
